TPU v7x, 512 devices: a whole 4x4x16 slice. The times are simulated.
512 devices in a mesh: seq: 128 (over y, z, x_lo), head: 4 (over x_hi, core).
Axes of the slice: x: 4 (x_hi: 2, x_lo: 2; x = x_hi * 2 + x_lo), y: 4, z: 16, core: 2. Of those that a mesh axis runs over, the one named last changes fastest.
Arguments:
- queries: bfloat16 [16384, 1024], P('seq', 'head'), may hold values from -16 to 16
- key_vectors: bfloat16 [16384, 1024], P('seq', 'head'), may hold values from -16 to 16
- values: bfloat16 [16384, 1024], P('seq', 'head'), may hold values from -6 to 6
- step_rates: float32 [16384, 4], P('seq', 'head'), may hold values from 0.1 to 1
- fast_weights: float32 [4, 3, 256, 256], P('head', None, 'seq'), may hold values from -0.375 to 0.375
- momentum: float32 [4, 3, 256, 256], P('head', None, 'seq'), may hold values from -0.4375 to 0.4375
- momentum_decay: float32 [4], P('head'), may hold values from 0.5 to 0.95
- memory_gain: float32 [1024], P('head'), may hold values from 0.5 to 1.5
- window_gain: float32 [1024], P('head'), may hold values from 0.5 to 1.5
Outputs:
- blended: bfloat16 [16384, 1024], P('seq', 'head')
- new_weights: float32 [4, 3, 256, 256], P('head', None, 'seq')
- new_momentum: float32 [4, 3, 256, 256], P('head', None, 'seq')
All inputs are finite; a program needn't handle non-finite values.
Results may differ from a plain program's by a relative error of at most 0.0085.
Values may be sent and summed in bfloat16 or wider, within the bound.
No kernel may reach another device: no remote copies, remote signals or barrier semaphores. Data moves between devices by JAX's collectives and lax.ppermute only.
A program may use at most 64 MiB of HBM per device.

v0:
```python
import math

import jax
import jax.numpy as jnp
from jax import lax
from jax.experimental import pallas as pl
from jax.experimental.pallas import tpu as pltpu
from jax.sharding import PartitionSpec as P


WINDOW = 512
Y_SIZE, Z_SIZE, X_SIZE = 4, 16, 2
NEAR_Z = 2
FAR = Z_SIZE // NEAR_Z
NEAR = Y_SIZE * NEAR_Z * X_SIZE
WIDTH = 256
ROW = 6 * WIDTH
TOKENS_HERE = 128
BACK = WINDOW // TOKENS_HERE


def place(y, z, x):
    return (y * Z_SIZE + z) * X_SIZE + x


NEAR_GROUPS = [
    [
        place(y, k * NEAR_Z + p, x)
        for y in range(Y_SIZE)
        for p in range(NEAR_Z)
        for x in range(X_SIZE)
    ]
    for k in range(FAR)
]
FAR_GROUPS = [
    [place(y, k * NEAR_Z + p, x) for k in range(FAR)]
    for y in range(Y_SIZE)
    for p in range(NEAR_Z)
    for x in range(X_SIZE)
]


def exchange(blocks, groups):
    return lax.all_to_all(blocks, "seq", 0, 0, axis_index_groups=groups, tiled=True)


def row_order():
    column = lax.broadcasted_iota(jnp.int32, (WIDTH, WIDTH), 1)
    row = lax.broadcasted_iota(jnp.int32, (WIDTH, WIDTH), 0)
    half, slot = column // 128, column % 128
    near, far = slot // FAR, slot % FAR
    x = near % X_SIZE
    p = (near // X_SIZE) % NEAR_Z
    y = near // (X_SIZE * NEAR_Z)
    device = (y * Z_SIZE + far * NEAR_Z + p) * X_SIZE + x
    return (row == 2 * device + half).astype(jnp.bfloat16)


def matmul(left, right):
    return jnp.dot(left, right, preferred_element_type=jnp.float32)


def matrix_of(whole, index):
    first = whole[:, index * 512 : index * 512 + 256]
    second = whole[:, index * 512 + 256 : index * 512 + 512]
    return jnp.concatenate([first, second], axis=0)


def silu_slope(field, sigmoid_x):
    return sigmoid_x * (1.0 + field * (1.0 - sigmoid_x))


def row_rms(field):
    return jnp.sqrt(jnp.mean(field * field, axis=-1, keepdims=True) + 1e-06)


def rms_scale(field, gain):
    return field * lax.rsqrt(jnp.mean(field * field, axis=-1, keepdims=True) + 1e-06) * gain


def contract_rows(left, right):
    return lax.dot_general(
        left, right, (((0,), (0,)), ((), ())), preferred_element_type=jnp.float32
    )


def contract_columns(left, right):
    return lax.dot_general(
        left, right, (((1,), (1,)), ((), ())), preferred_element_type=jnp.float32
    )


def flat_rows(ref):
    return jnp.concatenate([ref[m, e : e + 1, :] for m in range(3) for e in range(2)], axis=1)


def pack_kernel(weights_ref, moments_ref, out_ref):
    both = jnp.concatenate([flat_rows(weights_ref), flat_rows(moments_ref)], axis=0)
    out_ref[...] = jnp.broadcast_to(both.astype(jnp.bfloat16)[None], out_ref.shape)


def relay_kernel(line_ref, spread_ref, kept_ref):
    line = line_ref[...].astype(jnp.float32)
    weights, moments = line[:, 0, :], line[:, 1, :]
    kept_ref[:, :ROW] = weights
    kept_ref[:, ROW:] = moments
    weights = weights.astype(jnp.bfloat16)
    for slot in range(NEAR):
        spread_ref[slot] = weights


def gradient_kernel(rate, keys_ref, values_ref, rates_ref, whole_ref, out_ref):
    order = row_order()
    keys = matmul(keys_ref[...], order).astype(jnp.bfloat16)
    target_grad = (-(rate * rates_ref[...]) * values_ref[...].astype(jnp.float32)).astype(
        jnp.bfloat16
    )
    gate_pre = matmul(keys, matrix_of(whole_ref, 0))
    up_pre = matmul(keys, matrix_of(whole_ref, 1))
    down = matmul(order, matrix_of(whole_ref, 2)).astype(jnp.bfloat16)
    sigmoid_x = jax.nn.sigmoid(gate_pre)
    gate_act = gate_pre * sigmoid_x
    hidden = (gate_act * up_pre).astype(jnp.bfloat16)
    hidden_grad = contract_columns(target_grad, down)
    gate_grad = (hidden_grad * up_pre * silu_slope(gate_pre, sigmoid_x)).astype(jnp.bfloat16)
    up_grad = (hidden_grad * gate_act).astype(jnp.bfloat16)
    hidden = matmul(hidden, order).astype(jnp.bfloat16)
    pairs = ((keys, gate_grad), (keys, up_grad), (hidden, target_grad))
    for index, (left, right) in enumerate(pairs):
        part = contract_rows(left, right).astype(jnp.bfloat16)
        out_ref[:, index * 512 : index * 512 + 256] = part[:128]
        out_ref[:, index * 512 + 256 : index * 512 + 512] = part[128:]


def near_sum_kernel(parts_ref, out_ref):
    total = parts_ref[0].astype(jnp.float32)
    for slot in range(1, NEAR):
        total += parts_ref[slot].astype(jnp.float32)
    total = total.astype(jnp.bfloat16)
    for slot in range(FAR):
        out_ref[slot] = total


def update_kernel(
    far_ref, decay_ref, parts_ref, kept_ref, weights_ref, moments_ref,
    spread_ref, weights_out, moments_out, gradient_ref,
):
    gradient = parts_ref[0].astype(jnp.float32)
    for slot in range(1, FAR):
        gradient += parts_ref[slot].astype(jnp.float32)
    gradient_ref[...] = gradient
    decay = decay_ref[0]
    pieces = []
    for index in range(6):
        columns = slice(index * WIDTH, (index + 1) * WIDTH)
        weights = kept_ref[:, columns]
        moments = kept_ref[:, ROW + index * WIDTH : ROW + (index + 1) * WIDTH]
        candidate = weights - (decay * moments + gradient[:, columns])
        pieces.append(candidate * (row_rms(weights) / row_rms(candidate)))
    renewed = jnp.concatenate(pieces, axis=1).astype(jnp.bfloat16)
    for slot in range(NEAR):
        spread_ref[slot] = renewed
    own = gradient_ref[pl.ds(far_ref[0], 1), :]
    for m in range(3):
        for e in range(2):
            index = 2 * m + e
            weights = weights_ref[m, e : e + 1, :]
            moved = decay * moments_ref[m, e : e + 1, :] + own[:, index * WIDTH : (index + 1) * WIDTH]
            candidate = weights - moved
            moments_out[m, e : e + 1, :] = moved
            weights_out[m, e : e + 1, :] = candidate * (row_rms(weights) / row_rms(candidate))


def attention_kernel(index_ref, queries_ref, keys_ref, values_ref, gain_ref, *rest):
    earlier, out_ref = rest[:BACK], rest[BACK]
    queries = queries_ref[...]
    my_index = index_ref[0]
    query = lax.broadcasted_iota(jnp.int32, (TOKENS_HERE, TOKENS_HERE), 0)
    key = lax.broadcasted_iota(jnp.int32, (TOKENS_HERE, TOKENS_HERE), 1)
    scores = []
    for piece, back in zip(earlier, range(BACK, 0, -1)):
        part = contract_columns(queries, piece[:TOKENS_HERE, :]) * WIDTH ** (-0.5)
        allowed = jnp.broadcast_to(my_index, key.shape) >= back
        if back == BACK:
            allowed = allowed & (key > query)
        scores.append(jnp.where(allowed, part, jnp.float32(-1e30)))
    part = contract_columns(queries, keys_ref[...]) * WIDTH ** (-0.5)
    scores.append(jnp.where(key <= query, part, jnp.float32(-1e30)))
    scores = jnp.concatenate(scores, axis=1)
    weights = jnp.exp(scores - jnp.max(scores, axis=1, keepdims=True))
    chances = (weights / jnp.sum(weights, axis=1, keepdims=True)).astype(jnp.bfloat16)
    context = jnp.concatenate([piece[TOKENS_HERE:, :] for piece in earlier] + [values_ref[...]], axis=0)
    out_ref[...] = rms_scale(matmul(chances, context), gain_ref[...])


def recall_kernel(queries_ref, whole_ref, attended_ref, gain_ref, out_ref):
    order = row_order()
    queries = matmul(queries_ref[...], order).astype(jnp.bfloat16)
    gate_out = matmul(queries, matrix_of(whole_ref, 0))
    up_out = matmul(queries, matrix_of(whole_ref, 1))
    inner_act = (gate_out * jax.nn.sigmoid(gate_out) * up_out).astype(jnp.bfloat16)
    inner_act = matmul(inner_act, order).astype(jnp.bfloat16)
    recalled = matmul(inner_act, matrix_of(whole_ref, 2))
    out_ref[...] = (rms_scale(recalled, gain_ref[...]) + attended_ref[...]).astype(jnp.bfloat16)


VMEM = pl.BlockSpec(memory_space=pltpu.VMEM)
SMEM = pl.BlockSpec(memory_space=pltpu.SMEM)


def call(kernel, outputs, specs, *arrays, scratch=(), flops=10**8):
    single = not isinstance(outputs, list)
    shapes = [jax.ShapeDtypeStruct(*output) for output in ([outputs] if single else outputs)]
    moved = sum(array.size * array.dtype.itemsize for array in arrays)
    result = pl.pallas_call(
        kernel,
        out_shape=shapes,
        in_specs=specs,
        out_specs=[VMEM] * len(shapes),
        scratch_shapes=scratch,
        compiler_params=pltpu.CompilerParams(vmem_limit_bytes=8 * 2**20),
        cost_estimate=pl.CostEstimate(flops=flops, bytes_accessed=moved, transcendentals=0),
    )(*arrays)
    return result[0] if single else result


def per_device(
    queries,
    key_vectors,
    values,
    step_rates,
    fast_weights,
    momentum,
    momentum_decay,
    memory_gain,
    window_gain,
):
    seq_count = lax.axis_size("seq")
    my_index = lax.axis_index("seq")
    my_far = ((my_index // X_SIZE) % Z_SIZE) // NEAR_Z
    inner_rate = 0.1 / math.sqrt(TOKENS_HERE * seq_count)
    own_weights, own_moments = fast_weights[0], momentum[0]
    bf16, f32 = jnp.bfloat16, jnp.float32

    packed = call(pack_kernel, ((FAR, 2, ROW), bf16), [VMEM] * 2, own_weights, own_moments)
    line = exchange(packed, FAR_GROUPS)
    sent, kept = call(relay_kernel, [((NEAR, FAR, ROW), bf16), ((FAR, 2 * ROW), f32)], [VMEM], line)
    whole = exchange(sent, NEAR_GROUPS).reshape(seq_count, ROW)
    partial = call(
        lambda *refs: gradient_kernel(inner_rate, *refs),
        ((seq_count, ROW), bf16),
        [VMEM] * 4,
        key_vectors, values, step_rates, whole,
    )
    near_parts = exchange(partial.reshape(NEAR, FAR, ROW), NEAR_GROUPS)
    near_sum = call(near_sum_kernel, ((FAR, FAR, ROW), bf16), [VMEM], near_parts)
    far_parts = exchange(near_sum, FAR_GROUPS)
    renewed, weight_new, moment_new = call(
        update_kernel,
        [((NEAR, FAR, ROW), bf16), ((3, 2, WIDTH), f32), ((3, 2, WIDTH), f32)],
        [SMEM, SMEM] + [VMEM] * 4,
        my_far.reshape(1), momentum_decay, far_parts, kept, own_weights, own_moments,
        scratch=[pltpu.VMEM((FAR, ROW), f32)],
    )
    updated = exchange(renewed, NEAR_GROUPS).reshape(seq_count, ROW)
    both = jnp.concatenate([key_vectors, values], axis=0)
    earlier = []
    for back in range(BACK, 0, -1):
        pairs = [(i, i + back) for i in range(seq_count - back)]
        earlier.append(lax.ppermute(both, "seq", pairs))
    attended = call(
        attention_kernel,
        ((TOKENS_HERE, WIDTH), f32),
        [SMEM] + [VMEM] * (4 + BACK),
        my_index.reshape(1), queries, key_vectors, values,
        window_gain.reshape(1, WIDTH), *earlier,
    )
    blended = call(
        recall_kernel,
        ((TOKENS_HERE, WIDTH), bf16),
        [VMEM] * 4,
        queries, updated, attended, memory_gain.reshape(1, WIDTH),
    )
    return blended, weight_new[None], moment_new[None]


def solution(mesh):
    in_specs = (
        P("seq", "head"),
        P("seq", "head"),
        P("seq", "head"),
        P("seq", "head"),
        P("head", None, "seq", None),
        P("head", None, "seq", None),
        P("head"),
        P("head"),
        P("head"),
    )
    out_specs = (P("seq", "head"), P("head", None, "seq", None), P("head", None, "seq", None))
    return jax.shard_map(
        per_device, mesh=mesh, in_specs=in_specs, out_specs=out_specs, check_vma=False
    )
```

profile of v0, /device:TPU:8, one launch (start us, length us, event | category | flops | bytes accessed | tf_op | source)
XLA Modules:
  0.0 105.7 jit_solution(6257448040520422921)
XLA Ops:
  0.6 0.0 copy-start.5
  0.6 0.7 copy-done.5
  1.3 0.0 copy-start.7
  1.3 0.7 copy-done.7
  2.0 28.0 %all_to_all.25.line_ref = bf16[8,2,1536]{2,1,0:T(2,128)(2,1)S(1)} all-to-all(bf16[8,2,1536]{2,1,0:T(2,128)(2,1)S(1)} %shard_map.112), channel_id=1, replica_groups={{0,16,32,48,64,80,96,112},{4,20,36,52,68,84,100,116},{8,24,40,56,72,88,..., dimensions={0} | all-to-all | bytes 98304 | tf_op jit(solution)/shard_map/all_to_all | solution.py:44
  30.1 0.8 shard_map.113
  30.9 0.0 copy-start.9
  30.9 0.0 copy-start.1
  30.9 6.4 %all-to-all-start.1 = ((bf16[16,8,1536]{2,1,0:T(8,128)(2,1)}), bf16[16,8,1536]{2,1,0:T(8,128)(2,1)S(1)}, u32[]{:S(2)}, u32[]{:S(2)}) async-start(bf16[16,8,1536]{2,1,0:T(8,128)(2,1)} %get-tuple-element.8), calls=%async_computation.1 | async-start | bytes 786432 | tf_op jit(solution)/shard_map/all_to_all | solution.py:44
  37.3 0.0 copy-done.9
  37.4 0.0 copy-start
  37.4 0.1 copy.12.refs_2_
  37.5 6.8 %all-to-all-done.1 = bf16[16,8,1536]{2,1,0:T(8,128)(2,1)S(1)} async-done(((bf16[16,8,1536]{2,1,0:T(8,128)(2,1)}), bf16[16,8,1536]{2,1,0:T(8,128)(2,1)S(1)}, u32[]{:S(2)}, u32[]{:S(2)}) %all-to-all-start.1) | async-done | bytes 393248 | tf_op jit(solution)/shard_map/all_to_all | solution.py:44
  44.3 0.0 copy-done.1
  44.3 0.0 copy-done
  44.3 0.8 shard_map.114
  45.1 11.4 %all_to_all.26.parts_ref = bf16[16,8,1536]{2,1,0:T(8,128)(2,1)S(1)} all-to-all(bf16[16,8,1536]{2,1,0:T(8,128)(2,1)S(1)} %bitcast.13), channel_id=1, replica_groups={{0,4,8,12,128,132,136,140,256,260,264,268,384,388,392,396},{16,20,24,28..., dimensions={0} | all-to-all | bytes 786432 | tf_op jit(solution)/shard_map/all_to_all | solution.py:44
  56.6 0.7 shard_map.115
  57.3 3.4 %all-to-all-start.3 = ((bf16[8,8,1536]{2,1,0:T(8,128)(2,1)}), bf16[8,8,1536]{2,1,0:T(8,128)(2,1)S(1)}, u32[]{:S(2)}, u32[]{:S(2)}) async-start(bf16[8,8,1536]{2,1,0:T(8,128)(2,1)} %shard_map.115), calls=%async_computation.3 | async-start | bytes 393216 | tf_op jit(solution)/shard_map/all_to_all | solution.py:44
  60.7 0.0 copy-start.8
  60.7 0.0 copy-start.6
  61.4 15.0 %all-to-all-done.3.parts_ref = bf16[8,8,1536]{2,1,0:T(8,128)(2,1)S(1)} async-done(((bf16[8,8,1536]{2,1,0:T(8,128)(2,1)}), bf16[8,8,1536]{2,1,0:T(8,128)(2,1)S(1)}, u32[]{:S(2)}, u32[]{:S(2)}) %all-to-all-start.3) | async-done | bytes 196640 | tf_op jit(solution)/shard_map/all_to_all | solution.py:44
  76.4 0.0 copy-done.8
  76.4 0.0 copy-done.6
  76.4 0.9 shard_map.116
  77.3 4.8 %all-to-all-start.4 = ((bf16[16,8,1536]{2,1,0:T(8,128)(2,1)}), bf16[16,8,1536]{2,1,0:T(8,128)(2,1)S(1)}, u32[]{:S(2)}, u32[]{:S(2)}) async-start(bf16[16,8,1536]{2,1,0:T(8,128)(2,1)} %get-tuple-element.10), calls=%async_computation.4 | async-start | bytes 786432 | tf_op jit(solution)/shard_map/all_to_all | solution.py:44
  82.1 0.0 copy-start.2
  82.1 2.8 %collective-permute-start = (bf16[256,256]{1,0:T(8,128)(2,1)S(1)}, bf16[256,256]{1,0:T(8,128)(2,1)S(1)}, u32[]{:S(2)}, u32[]{:S(2)}) collective-permute-start(bf16[256,256]{1,0:T(8,128)(2,1)S(1)} %constant_dynamic-update-slice_fusion), channel_id=1, source_target_pairs={{0,16},{4,20},{8,24},{12,28},{16,32},{20,36},{24,40},{28,44},{32,4... | collective-permute-start | bytes 393224 | tf_op jit(solution)/shard_map/ppermute | solution.py:270
  85.0 4.3 %collective-permute-start.1 = (bf16[256,256]{1,0:T(8,128)(2,1)S(1)}, bf16[256,256]{1,0:T(8,128)(2,1)S(1)}, u32[]{:S(2)}, u32[]{:S(2)}) collective-permute-start(bf16[256,256]{1,0:T(8,128)(2,1)S(1)} %constant_dynamic-update-slice_fusion), channel_id=1, source_target_pairs={{0,12},{4,16},{8,20},{12,24},{16,28},{20,32},{24,36},{28,40},{32,4... | collective-permute-start | bytes 393224 | tf_op jit(solution)/shard_map/ppermute | solution.py:270
  89.3 1.9 %collective-permute-start.2 = (bf16[256,256]{1,0:T(8,128)(2,1)S(1)}, bf16[256,256]{1,0:T(8,128)(2,1)S(1)}, u32[]{:S(2)}, u32[]{:S(2)}) collective-permute-start(bf16[256,256]{1,0:T(8,128)(2,1)S(1)} %constant_dynamic-update-slice_fusion), channel_id=1, source_target_pairs={{0,8},{4,12},{8,16},{12,20},{16,24},{20,28},{24,32},{28,36},{32,40... | collective-permute-start | bytes 393224 | tf_op jit(solution)/shard_map/ppermute | solution.py:270
  91.2 2.8 %collective-permute-start.3 = (bf16[256,256]{1,0:T(8,128)(2,1)S(1)}, bf16[256,256]{1,0:T(8,128)(2,1)S(1)}, u32[]{:S(2)}, u32[]{:S(2)}) collective-permute-start(bf16[256,256]{1,0:T(8,128)(2,1)S(1)} %constant_dynamic-update-slice_fusion), channel_id=1, source_target_pairs={{0,4},{4,8},{8,12},{12,16},{16,20},{20,24},{24,28},{28,32},{32,36}... | collective-permute-start | bytes 393224 | tf_op jit(solution)/shard_map/ppermute | solution.py:270
  94.0 0.4 collective-permute-done.rest_0_
  94.4 5.3 %collective-permute-done.1.rest_1_ = bf16[256,256]{1,0:T(8,128)(2,1)S(1)} collective-permute-done((bf16[256,256]{1,0:T(8,128)(2,1)S(1)}, bf16[256,256]{1,0:T(8,128)(2,1)S(1)}, u32[]{:S(2)}, u32[]{:S(2)}) %collective-permute-start.1) | collective-permute-done | bytes 131104 | tf_op jit(solution)/shard_map/ppermute | solution.py:270
  99.7 0.0 collective-permute-done.2.rest_2_
  99.7 2.5 %collective-permute-done.3.rest_3_ = bf16[256,256]{1,0:T(8,128)(2,1)S(1)} collective-permute-done((bf16[256,256]{1,0:T(8,128)(2,1)S(1)}, bf16[256,256]{1,0:T(8,128)(2,1)S(1)}, u32[]{:S(2)}, u32[]{:S(2)}) %collective-permute-start.3) | collective-permute-done | bytes 131104 | tf_op jit(solution)/shard_map/ppermute | solution.py:270
  102.2 0.0 copy-start.3
  102.2 0.0 copy-done.2
  102.2 0.7 copy-done.3
  102.9 0.8 shard_map.117.attended_ref
  103.7 0.0 all-to-all-done.4
  103.7 0.0 copy-start.4
  103.7 0.7 copy-done.4
  104.4 1.3 %shard_map.118 = bf16[128,256]{1,0:T(8,128)(2,1)} custom-call(bf16[128,256]{1,0:T(8,128)(2,1)S(1)} %copy-done.2, bf16[128,1536]{1,0:T(8,128)(2,1)S(1)} %bitcast.11, f32[128,256]{1,0:T(8,128)S(1)} %shard_map.117.attended_ref, f32[1,256]{1,0:T(1,128)S(1)} %bitcast.15), custom_call_target="tpu_custom_call" | custom-call | flops 100000000 | bytes 590848 | tf_op jit(solution)/shard_map/pallas_call | solution.py:215
  (3 shorter events, 0.0 us)
Async XLA Ops:
  0.6 0.7 copy-start.5
  1.3 0.7 copy-start.7
  30.9 6.4 %copy-start.9 = (f32[128,1]{0,1:T(1,128)S(1)}, f32[128,1]{0,1:T(1,128)}, u32[]{:S(2)}) copy-start(f32[128,1]{0,1:T(1,128)} %param.12) | copy-start | bytes 1540
  30.9 13.4 %copy-start.1 = (bf16[128,256]{1,0:T(8,128)(2,1)S(1)}, bf16[128,256]{1,0:T(8,128)(2,1)}, u32[]{:S(2)}) copy-start(bf16[128,256]{1,0:T(8,128)(2,1)} %values_ref.1) | copy-start | bytes 196612
  30.9 13.4 %all-to-all-start.1 = ((bf16[16,8,1536]{2,1,0:T(8,128)(2,1)}), bf16[16,8,1536]{2,1,0:T(8,128)(2,1)S(1)}, u32[]{:S(2)}, u32[]{:S(2)}) async-start(bf16[16,8,1536]{2,1,0:T(8,128)(2,1)} %get-tuple-element.8), calls=%async_computation.1 | async-start | bytes 786432 | tf_op jit(solution)/shard_map/all_to_all | solution.py:44
  37.4 6.9 %copy-start = (bf16[128,256]{1,0:T(8,128)(2,1)S(1)}, bf16[128,256]{1,0:T(8,128)(2,1)}, u32[]{:S(2)}) copy-start(bf16[128,256]{1,0:T(8,128)(2,1)} %keys_ref.1) | copy-start | bytes 196612
  57.3 19.1 %all-to-all-start.3 = ((bf16[8,8,1536]{2,1,0:T(8,128)(2,1)}), bf16[8,8,1536]{2,1,0:T(8,128)(2,1)S(1)}, u32[]{:S(2)}, u32[]{:S(2)}) async-start(bf16[8,8,1536]{2,1,0:T(8,128)(2,1)} %shard_map.115), calls=%async_computation.3 | async-start | bytes 393216 | tf_op jit(solution)/shard_map/all_to_all | solution.py:44
  60.7 15.7 %copy-start.8 = (f32[1,3,2,256]{3,2,1,0:T(2,128)S(1)}, f32[1,3,2,256]{3,2,1,0:T(2,128)}, u32[]{:S(2)}) copy-start(f32[1,3,2,256]{3,2,1,0:T(2,128)} %param.14) | copy-start | bytes 18436
  60.7 15.6 %copy-start.6 = (f32[1,3,2,256]{3,2,1,0:T(2,128)S(1)}, f32[1,3,2,256]{3,2,1,0:T(2,128)}, u32[]{:S(2)}) copy-start(f32[1,3,2,256]{3,2,1,0:T(2,128)} %param.13) | copy-start | bytes 18436
  77.3 26.4 %all-to-all-start.4 = ((bf16[16,8,1536]{2,1,0:T(8,128)(2,1)}), bf16[16,8,1536]{2,1,0:T(8,128)(2,1)S(1)}, u32[]{:S(2)}, u32[]{:S(2)}) async-start(bf16[16,8,1536]{2,1,0:T(8,128)(2,1)} %get-tuple-element.10), calls=%async_computation.4 | async-start | bytes 786432 | tf_op jit(solution)/shard_map/all_to_all | solution.py:44
  82.1 20.1 %copy-start.2 = (bf16[128,256]{1,0:T(8,128)(2,1)S(1)}, bf16[128,256]{1,0:T(8,128)(2,1)}, u32[]{:S(2)}) copy-start(bf16[128,256]{1,0:T(8,128)(2,1)} %queries_ref.3) | copy-start | bytes 196612
  82.1 12.3 %collective-permute-start = (bf16[256,256]{1,0:T(8,128)(2,1)S(1)}, bf16[256,256]{1,0:T(8,128)(2,1)S(1)}, u32[]{:S(2)}, u32[]{:S(2)}) collective-permute-start(bf16[256,256]{1,0:T(8,128)(2,1)S(1)} %constant_dynamic-update-slice_fusion), channel_id=1, source_target_pairs={{0,16},{4,20},{8,24},{12,28},{16,32},{20,36},{24,40},{28,44},{32,4... | collective-permute-start | bytes 393224 | tf_op jit(solution)/shard_map/ppermute | solution.py:270
  85.0 14.8 %collective-permute-start.1 = (bf16[256,256]{1,0:T(8,128)(2,1)S(1)}, bf16[256,256]{1,0:T(8,128)(2,1)S(1)}, u32[]{:S(2)}, u32[]{:S(2)}) collective-permute-start(bf16[256,256]{1,0:T(8,128)(2,1)S(1)} %constant_dynamic-update-slice_fusion), channel_id=1, source_target_pairs={{0,12},{4,16},{8,20},{12,24},{16,28},{20,32},{24,36},{28,40},{32,4... | collective-permute-start | bytes 393224 | tf_op jit(solution)/shard_map/ppermute | solution.py:270
  89.3 10.5 %collective-permute-start.2 = (bf16[256,256]{1,0:T(8,128)(2,1)S(1)}, bf16[256,256]{1,0:T(8,128)(2,1)S(1)}, u32[]{:S(2)}, u32[]{:S(2)}) collective-permute-start(bf16[256,256]{1,0:T(8,128)(2,1)S(1)} %constant_dynamic-update-slice_fusion), channel_id=1, source_target_pairs={{0,8},{4,12},{8,16},{12,20},{16,24},{20,28},{24,32},{28,36},{32,40... | collective-permute-start | bytes 393224 | tf_op jit(solution)/shard_map/ppermute | solution.py:270
  91.2 11.0 %collective-permute-start.3 = (bf16[256,256]{1,0:T(8,128)(2,1)S(1)}, bf16[256,256]{1,0:T(8,128)(2,1)S(1)}, u32[]{:S(2)}, u32[]{:S(2)}) collective-permute-start(bf16[256,256]{1,0:T(8,128)(2,1)S(1)} %constant_dynamic-update-slice_fusion), channel_id=1, source_target_pairs={{0,4},{4,8},{8,12},{12,16},{16,20},{20,24},{24,28},{28,32},{32,36}... | collective-permute-start | bytes 393224 | tf_op jit(solution)/shard_map/ppermute | solution.py:270
  102.2 0.7 copy-start.3
  103.7 0.7 copy-start.4
where the time goes:
time: 106 us
  blocking collectives  39.5 us (37%)
  waiting for transfers between devices  30 us (28%)
  starting transfers between devices  26.4 us (25%)
  Pallas kernels  5.37 us (5%)
  local copies, waits for them, and re-layouts  2.89 us (3%)
  between operations  1.47 us (1%)
    all_to_all x2, blocking collectives, exchange(): lax.all_to_all(blocks, 'seq', 0, 0, axis_index_groups=groups, tiled=True)  39.5 us
    all_to_all x3, waiting for transfers between devices, exchange(): lax.all_to_all(blocks, 'seq', 0, 0, axis_index_groups=groups, tiled=True)  21.8 us
    all_to_all x3, starting transfers between devices, exchange(): lax.all_to_all(blocks, 'seq', 0, 0, axis_index_groups=groups, tiled=True)  14.6 us
    ppermute x4, starting transfers between devices, per_device(): earlier.append(lax.ppermute(both, 'seq', pairs))  11.8 us
    ppermute x4, waiting for transfers between devices, per_device(): earlier.append(lax.ppermute(both, 'seq', pairs))  8.25 us
    pallas_call x7, Pallas kernels, call(): pl.pallas_call(kernel, out_shape=shapes, in_specs=specs, out_specs=[VMEM]...  5.37 us
    unnamed x22, local copies, waits for them, and re-layouts  2.88 us
  transfers between devices with their start and end apart: 7, of which 5 were waited for; matrix products, arithmetic and copies ran while one was open for 0% of the time, Pallas kernels for 1%

commit v1 on v0

--- a/solution.py
+++ b/solution.py
@@ -94,9 +94,37 @@
     return jnp.concatenate([ref[m, e : e + 1, :] for m in range(3) for e in range(2)], axis=1)
 
 
-def pack_kernel(weights_ref, moments_ref, out_ref):
+def pack_kernel(
+    weights_hbm, moments_hbm, keys_hbm, values_hbm, memory_hbm, window_hbm,
+    out_ref, both_ref, weights_ref, moments_ref, memory_ref, window_ref, sems,
+):
+    moves = (
+        (weights_hbm, weights_ref),
+        (moments_hbm, moments_ref),
+        (keys_hbm, both_ref.at[pl.ds(0, TOKENS_HERE)]),
+        (values_hbm, both_ref.at[pl.ds(TOKENS_HERE, TOKENS_HERE)]),
+        (memory_hbm, memory_ref),
+        (window_hbm, window_ref),
+    )
+    copies = [
+        pltpu.make_async_copy(source, target, sems.at[i])
+        for i, (source, target) in enumerate(moves)
+    ]
+    for copy in copies:
+        copy.start()
+    copies[0].wait()
+    copies[1].wait()
     both = jnp.concatenate([flat_rows(weights_ref), flat_rows(moments_ref)], axis=0)
     out_ref[...] = jnp.broadcast_to(both.astype(jnp.bfloat16)[None], out_ref.shape)
+    for copy in copies[2:]:
+        copy.wait()
+
+
+def prepare_kernel(rate, both_ref, rates_ref, keys_out, target_out):
+    keys_out[...] = matmul(both_ref[:TOKENS_HERE, :], row_order()).astype(jnp.bfloat16)
+    rates = jnp.transpose(jnp.broadcast_to(rates_ref[...], (TOKENS_HERE, TOKENS_HERE)))
+    scale = -(rate * jnp.concatenate([rates, rates], axis=1))
+    target_out[...] = (scale * both_ref[TOKENS_HERE:, :].astype(jnp.float32)).astype(jnp.bfloat16)
 
 
 def relay_kernel(line_ref, spread_ref, kept_ref):
@@ -109,12 +137,9 @@
         spread_ref[slot] = weights
 
 
-def gradient_kernel(rate, keys_ref, values_ref, rates_ref, whole_ref, out_ref):
+def gradient_kernel(keys_ref, target_ref, whole_ref, out_ref):
     order = row_order()
-    keys = matmul(keys_ref[...], order).astype(jnp.bfloat16)
-    target_grad = (-(rate * rates_ref[...]) * values_ref[...].astype(jnp.float32)).astype(
-        jnp.bfloat16
-    )
+    keys, target_grad = keys_ref[...], target_ref[...]
     gate_pre = matmul(keys, matrix_of(whole_ref, 0))
     up_pre = matmul(keys, matrix_of(whole_ref, 1))
     down = matmul(order, matrix_of(whole_ref, 2)).astype(jnp.bfloat16)
@@ -141,10 +166,7 @@
         out_ref[slot] = total
 
 
-def update_kernel(
-    far_ref, decay_ref, parts_ref, kept_ref, weights_ref, moments_ref,
-    spread_ref, weights_out, moments_out, gradient_ref,
-):
+def update_kernel(far_ref, decay_ref, parts_ref, kept_ref, spread_ref, own_ref, gradient_ref):
     gradient = parts_ref[0].astype(jnp.float32)
     for slot in range(1, FAR):
         gradient += parts_ref[slot].astype(jnp.float32)
@@ -160,55 +182,86 @@
     renewed = jnp.concatenate(pieces, axis=1).astype(jnp.bfloat16)
     for slot in range(NEAR):
         spread_ref[slot] = renewed
-    own = gradient_ref[pl.ds(far_ref[0], 1), :]
+    own_ref[...] = gradient_ref[pl.ds(far_ref[0], 1), :]
+
+
+def attention_kernel(
+    index_ref, queries_ref, both_ref, second_ref, fourth_ref, swapped_ref, gain_ref,
+    out_ref, queries_out,
+):
+    queries = queries_ref[...]
+    queries_out[...] = matmul(queries, row_order()).astype(jnp.bfloat16)
+    my_index = index_ref[0]
+    query = lax.broadcasted_iota(jnp.int32, (TOKENS_HERE, TOKENS_HERE), 0)
+    key = lax.broadcasted_iota(jnp.int32, (TOKENS_HERE, TOKENS_HERE), 1)
+    pieces = (
+        (4, fourth_ref, 0),
+        (3, swapped_ref, 2 * TOKENS_HERE),
+        (2, second_ref, 0),
+        (1, swapped_ref, 0),
+        (0, both_ref, 0),
+    )
+    scores = []
+    for back, ref, first in pieces:
+        part = contract_columns(queries, ref[first : first + TOKENS_HERE, :]) * WIDTH ** (-0.5)
+        allowed = jnp.broadcast_to(my_index, key.shape) >= back
+        if back == BACK:
+            allowed = allowed & (key > query)
+        if back == 0:
+            allowed = key <= query
+        scores.append(jnp.where(allowed, part, jnp.float32(-1e30)))
+    scores = jnp.concatenate(scores, axis=1)
+    weights = jnp.exp(scores - jnp.max(scores, axis=1, keepdims=True))
+    chances = (weights / jnp.sum(weights, axis=1, keepdims=True)).astype(jnp.bfloat16)
+    context = jnp.concatenate(
+        [ref[first + TOKENS_HERE : first + 2 * TOKENS_HERE, :] for _, ref, first in pieces], axis=0
+    )
+    out_ref[...] = rms_scale(matmul(chances, context), gain_ref[...])
+
+
+def recall_kernel(
+    decay_ref, own_ref, weights_ref, moments_ref, queries_ref, whole_ref, attended_ref, gain_ref,
+    out_hbm, weights_hbm, moments_hbm, out_ref, weights_out, moments_out, sems,
+):
+    decay = decay_ref[0]
     for m in range(3):
         for e in range(2):
-            index = 2 * m + e
+            first = (2 * m + e) * WIDTH
             weights = weights_ref[m, e : e + 1, :]
-            moved = decay * moments_ref[m, e : e + 1, :] + own[:, index * WIDTH : (index + 1) * WIDTH]
+            moved = decay * moments_ref[m, e : e + 1, :] + own_ref[:, first : first + WIDTH]
             candidate = weights - moved
             moments_out[m, e : e + 1, :] = moved
             weights_out[m, e : e + 1, :] = candidate * (row_rms(weights) / row_rms(candidate))
-
-
-def attention_kernel(index_ref, queries_ref, keys_ref, values_ref, gain_ref, *rest):
-    earlier, out_ref = rest[:BACK], rest[BACK]
+    state = [
+        pltpu.make_async_copy(weights_out, weights_hbm, sems.at[0]),
+        pltpu.make_async_copy(moments_out, moments_hbm, sems.at[1]),
+    ]
+    for copy in state:
+        copy.start()
     queries = queries_ref[...]
-    my_index = index_ref[0]
-    query = lax.broadcasted_iota(jnp.int32, (TOKENS_HERE, TOKENS_HERE), 0)
-    key = lax.broadcasted_iota(jnp.int32, (TOKENS_HERE, TOKENS_HERE), 1)
-    scores = []
-    for piece, back in zip(earlier, range(BACK, 0, -1)):
-        part = contract_columns(queries, piece[:TOKENS_HERE, :]) * WIDTH ** (-0.5)
-        allowed = jnp.broadcast_to(my_index, key.shape) >= back
-        if back == BACK:
-            allowed = allowed & (key > query)
-        scores.append(jnp.where(allowed, part, jnp.float32(-1e30)))
-    part = contract_columns(queries, keys_ref[...]) * WIDTH ** (-0.5)
-    scores.append(jnp.where(key <= query, part, jnp.float32(-1e30)))
-    scores = jnp.concatenate(scores, axis=1)
-    weights = jnp.exp(scores - jnp.max(scores, axis=1, keepdims=True))
-    chances = (weights / jnp.sum(weights, axis=1, keepdims=True)).astype(jnp.bfloat16)
-    context = jnp.concatenate([piece[TOKENS_HERE:, :] for piece in earlier] + [values_ref[...]], axis=0)
-    out_ref[...] = rms_scale(matmul(chances, context), gain_ref[...])
-
-
-def recall_kernel(queries_ref, whole_ref, attended_ref, gain_ref, out_ref):
-    order = row_order()
-    queries = matmul(queries_ref[...], order).astype(jnp.bfloat16)
     gate_out = matmul(queries, matrix_of(whole_ref, 0))
     up_out = matmul(queries, matrix_of(whole_ref, 1))
+    down = matmul(row_order(), matrix_of(whole_ref, 2)).astype(jnp.bfloat16)
     inner_act = (gate_out * jax.nn.sigmoid(gate_out) * up_out).astype(jnp.bfloat16)
-    inner_act = matmul(inner_act, order).astype(jnp.bfloat16)
-    recalled = matmul(inner_act, matrix_of(whole_ref, 2))
+    recalled = matmul(inner_act, down)
     out_ref[...] = (rms_scale(recalled, gain_ref[...]) + attended_ref[...]).astype(jnp.bfloat16)
+    last = pltpu.make_async_copy(out_ref, out_hbm, sems.at[2])
+    last.start()
+    for copy in state:
+        copy.wait()
+    last.wait()
 
 
 VMEM = pl.BlockSpec(memory_space=pltpu.VMEM)
 SMEM = pl.BlockSpec(memory_space=pltpu.SMEM)
-
-
-def call(kernel, outputs, specs, *arrays, scratch=(), flops=10**8):
+HBM = pl.BlockSpec(memory_space=pltpu.HBM)
+
+
+def stay(array):
+    return pltpu.with_memory_space_constraint(array, pltpu.HBM)
+
+
+def call(kernel, outputs, specs, *arrays, out_spec=VMEM, scratch=(), flops=10**8):
     single = not isinstance(outputs, list)
     shapes = [jax.ShapeDtypeStruct(*output) for output in ([outputs] if single else outputs)]
     moved = sum(array.size * array.dtype.itemsize for array in arrays)
@@ -216,7 +269,7 @@
         kernel,
         out_shape=shapes,
         in_specs=specs,
-        out_specs=[VMEM] * len(shapes),
+        out_specs=[out_spec] * len(shapes),
         scratch_shapes=scratch,
         compiler_params=pltpu.CompilerParams(vmem_limit_bytes=8 * 2**20),
         cost_estimate=pl.CostEstimate(flops=flops, bytes_accessed=moved, transcendentals=0),
@@ -239,47 +292,72 @@
     my_index = lax.axis_index("seq")
     my_far = ((my_index // X_SIZE) % Z_SIZE) // NEAR_Z
     inner_rate = 0.1 / math.sqrt(TOKENS_HERE * seq_count)
-    own_weights, own_moments = fast_weights[0], momentum[0]
     bf16, f32 = jnp.bfloat16, jnp.float32
-
-    packed = call(pack_kernel, ((FAR, 2, ROW), bf16), [VMEM] * 2, own_weights, own_moments)
+    block = ((3, 2, WIDTH), f32)
+    line_gain = ((1, WIDTH), f32)
+
+    packed, both, own_weights, own_moments, memory_row, window_row = call(
+        pack_kernel,
+        [((FAR, 2, ROW), bf16), ((2 * TOKENS_HERE, WIDTH), bf16), block, block, line_gain, line_gain],
+        [HBM] * 6,
+        *map(
+            stay,
+            (
+                fast_weights[0], momentum[0], key_vectors, values,
+                memory_gain.reshape(1, WIDTH), window_gain.reshape(1, WIDTH),
+            ),
+        ),
+        scratch=[pltpu.SemaphoreType.DMA((6,))],
+    )
     line = exchange(packed, FAR_GROUPS)
+    second = lax.ppermute(both, "seq", [(i, i + 2) for i in range(seq_count - 2)])
+    fourth = lax.ppermute(both, "seq", [(i, i + 4) for i in range(seq_count - 4)])
+    keys, target_grad = call(
+        lambda *refs: prepare_kernel(inner_rate, *refs),
+        [((TOKENS_HERE, WIDTH), bf16)] * 2,
+        [VMEM] * 2,
+        both, step_rates.reshape(1, TOKENS_HERE),
+    )
     sent, kept = call(relay_kernel, [((NEAR, FAR, ROW), bf16), ((FAR, 2 * ROW), f32)], [VMEM], line)
     whole = exchange(sent, NEAR_GROUPS).reshape(seq_count, ROW)
-    partial = call(
-        lambda *refs: gradient_kernel(inner_rate, *refs),
-        ((seq_count, ROW), bf16),
-        [VMEM] * 4,
-        key_vectors, values, step_rates, whole,
-    )
+    partial = call(gradient_kernel, ((seq_count, ROW), bf16), [VMEM] * 3, keys, target_grad, whole)
     near_parts = exchange(partial.reshape(NEAR, FAR, ROW), NEAR_GROUPS)
     near_sum = call(near_sum_kernel, ((FAR, FAR, ROW), bf16), [VMEM], near_parts)
     far_parts = exchange(near_sum, FAR_GROUPS)
-    renewed, weight_new, moment_new = call(
+    odd = lax.rem(my_index, 2) == 1
+    offered = jnp.where(
+        odd,
+        jnp.concatenate([second, fourth], axis=0),
+        jnp.concatenate([both, second], axis=0),
+    )
+    swapped = lax.ppermute(offered, "seq", [(i, i ^ 1) for i in range(seq_count)])
+    attended, queries_ordered = call(
+        attention_kernel,
+        [((TOKENS_HERE, WIDTH), f32), ((TOKENS_HERE, WIDTH), bf16)],
+        [SMEM] + [VMEM] * 6,
+        my_index.reshape(1), queries, both, second, fourth, swapped, window_row,
+    )
+    renewed, own_gradient = call(
         update_kernel,
-        [((NEAR, FAR, ROW), bf16), ((3, 2, WIDTH), f32), ((3, 2, WIDTH), f32)],
-        [SMEM, SMEM] + [VMEM] * 4,
-        my_far.reshape(1), momentum_decay, far_parts, kept, own_weights, own_moments,
+        [((NEAR, FAR, ROW), bf16), ((1, ROW), f32)],
+        [SMEM, SMEM] + [VMEM] * 2,
+        my_far.reshape(1), momentum_decay, far_parts, kept,
         scratch=[pltpu.VMEM((FAR, ROW), f32)],
     )
     updated = exchange(renewed, NEAR_GROUPS).reshape(seq_count, ROW)
-    both = jnp.concatenate([key_vectors, values], axis=0)
-    earlier = []
-    for back in range(BACK, 0, -1):
-        pairs = [(i, i + back) for i in range(seq_count - back)]
-        earlier.append(lax.ppermute(both, "seq", pairs))
-    attended = call(
-        attention_kernel,
-        ((TOKENS_HERE, WIDTH), f32),
-        [SMEM] + [VMEM] * (4 + BACK),
-        my_index.reshape(1), queries, key_vectors, values,
-        window_gain.reshape(1, WIDTH), *earlier,
-    )
-    blended = call(
+    blended, weight_new, moment_new = call(
         recall_kernel,
-        ((TOKENS_HERE, WIDTH), bf16),
-        [VMEM] * 4,
-        queries, updated, attended, memory_gain.reshape(1, WIDTH),
+        [((TOKENS_HERE, WIDTH), bf16), block, block],
+        [SMEM] + [VMEM] * 7,
+        momentum_decay, own_gradient, own_weights, own_moments,
+        queries_ordered, updated, attended, memory_row,
+        out_spec=HBM,
+        scratch=[
+            pltpu.VMEM((TOKENS_HERE, WIDTH), bf16),
+            pltpu.VMEM(*block),
+            pltpu.VMEM(*block),
+            pltpu.SemaphoreType.DMA((3,)),
+        ],
     )
     return blended, weight_new[None], moment_new[None]
 

time: 106 us -> 105 us (level)
  starting transfers between devices: 26.4 us -> 24 us
  waiting for transfers between devices: 30 us -> 32.4 us
  local copies, waits for them, and re-layouts: 2.89 us -> 0.66 us
    ppermute x4 -> x3, waiting for transfers between devices: 8.25 us -> 11.3 us  [the longest x1 4.89 us: per_device(): lax.ppermute(offered, 'seq', [(i, i ^ 1) for i in range(seq_count)])]
    ppermute x4 -> x3, starting transfers between devices: 11.8 us -> 9.58 us  [the longest x1 3.38 us: per_device(): lax.ppermute(both, 'seq', [(i, i + 2) for i in range(seq_count - 2)])]
    unnamed x22 -> x4, local copies, waits for them, and re-layouts: 2.88 us -> 0.66 us
    pallas_call x7 -> x8, Pallas kernels: 5.37 us -> 6.22 us  [call(): pl.pallas_call(kernel, out_shape=shapes, in_specs=specs, out_specs=[out_s...]
  transfers between devices with their start and end apart: 7 -> 6, of which waited for: 5 -> 5; matrix products, arithmetic and copies ran while one was open for 0% -> 0% of each run, Pallas kernels for 1% -> 1%
where the time goes in v1:
time: 105 us; the launch traced here: 104 us
  blocking collectives  39.5 us (38%)
  waiting for transfers between devices  32.4 us (31%)
  starting transfers between devices  24 us (23%)
  Pallas kernels  6.22 us (6%)
  between operations  1.41 us (1%)
    all_to_all x2, blocking collectives, exchange(): lax.all_to_all(blocks, 'seq', 0, 0, axis_index_groups=groups, tiled=True)  39.5 us
    all_to_all x3, waiting for transfers between devices, exchange(): lax.all_to_all(blocks, 'seq', 0, 0, axis_index_groups=groups, tiled=True)  21.1 us
    all_to_all x3, starting transfers between devices, exchange(): lax.all_to_all(blocks, 'seq', 0, 0, axis_index_groups=groups, tiled=True)  14.5 us
    pallas_call x8, Pallas kernels, call(): pl.pallas_call(kernel, out_shape=shapes, in_specs=specs, out_specs=[out_s...  6.22 us
    ppermute x1, waiting for transfers between devices, per_device(): lax.ppermute(offered, 'seq', [(i, i ^ 1) for i in range(seq_count)])  4.89 us
    ppermute x1, waiting for transfers between devices, per_device(): lax.ppermute(both, 'seq', [(i, i + 4) for i in range(seq_count - 4)])  4.68 us
    ppermute x1, starting transfers between devices, per_device(): lax.ppermute(both, 'seq', [(i, i + 2) for i in range(seq_count - 2)])  3.38 us
    ppermute x1, starting transfers between devices, per_device(): lax.ppermute(offered, 'seq', [(i, i ^ 1) for i in range(seq_count)])  3.37 us
  transfers between devices with their start and end apart: 6, of which 5 were waited for; matrix products, arithmetic and copies ran while one was open for 0% of the time, Pallas kernels for 1%

profile of v1, /device:TPU:8, one launch (start us, length us, event | category | flops | bytes accessed | tf_op | source)
XLA Modules:
  0.0 104.3 jit_solution(5459539818147541110)
XLA Ops:
  0.6 1.0 shard_map.112
  1.6 28.0 %all_to_all.25.line_ref = bf16[8,2,1536]{2,1,0:T(2,128)(2,1)S(1)} all-to-all(bf16[8,2,1536]{2,1,0:T(2,128)(2,1)S(1)} %get-tuple-element.23), channel_id=1, replica_groups={{0,16,32,48,64,80,96,112},{4,20,36,52,68,84,100,116},{8,24,40,56,72,88,..., dimensions={0} | all-to-all | bytes 98304 | tf_op jit(solution)/shard_map/all_to_all | solution.py:44
  29.6 0.8 shard_map.114
  30.5 6.3 %all-to-all-start.1 = ((bf16[16,8,1536]{2,1,0:T(8,128)(2,1)}), bf16[16,8,1536]{2,1,0:T(8,128)(2,1)S(1)}, u32[]{:S(2)}, u32[]{:S(2)}) async-start(bf16[16,8,1536]{2,1,0:T(8,128)(2,1)} %get-tuple-element.24), calls=%async_computation.1 | async-start | bytes 786432 | tf_op jit(solution)/shard_map/all_to_all | solution.py:44
  36.8 0.0 copy-start.1
  36.8 0.6 copy-done.1
  37.4 0.2 shard_map.113
  37.6 6.1 %all-to-all-done.1 = bf16[16,8,1536]{2,1,0:T(8,128)(2,1)S(1)} async-done(((bf16[16,8,1536]{2,1,0:T(8,128)(2,1)}), bf16[16,8,1536]{2,1,0:T(8,128)(2,1)S(1)}, u32[]{:S(2)}, u32[]{:S(2)}) %all-to-all-start.1) | async-done | bytes 393248 | tf_op jit(solution)/shard_map/all_to_all | solution.py:44
  43.7 0.7 shard_map.115
  44.4 11.4 %all_to_all.26.parts_ref = bf16[16,8,1536]{2,1,0:T(8,128)(2,1)S(1)} all-to-all(bf16[16,8,1536]{2,1,0:T(8,128)(2,1)S(1)} %bitcast.14), channel_id=1, replica_groups={{0,4,8,12,128,132,136,140,256,260,264,268,384,388,392,396},{16,20,24,28..., dimensions={0} | all-to-all | bytes 786432 | tf_op jit(solution)/shard_map/all_to_all | solution.py:44
  55.8 0.7 shard_map.116
  56.6 3.4 %all-to-all-start.3 = ((bf16[8,8,1536]{2,1,0:T(8,128)(2,1)}), bf16[8,8,1536]{2,1,0:T(8,128)(2,1)S(1)}, u32[]{:S(2)}, u32[]{:S(2)}) async-start(bf16[8,8,1536]{2,1,0:T(8,128)(2,1)} %shard_map.116), calls=%async_computation.3 | async-start | bytes 393216 | tf_op jit(solution)/shard_map/all_to_all | solution.py:44
  60.7 15.0 %all-to-all-done.3.parts_ref = bf16[8,8,1536]{2,1,0:T(8,128)(2,1)S(1)} async-done(((bf16[8,8,1536]{2,1,0:T(8,128)(2,1)}), bf16[8,8,1536]{2,1,0:T(8,128)(2,1)S(1)}, u32[]{:S(2)}, u32[]{:S(2)}) %all-to-all-start.3) | async-done | bytes 196640 | tf_op jit(solution)/shard_map/all_to_all | solution.py:44
  75.7 0.9 shard_map.117
  76.6 4.8 %all-to-all-start.4 = ((bf16[16,8,1536]{2,1,0:T(8,128)(2,1)}), bf16[16,8,1536]{2,1,0:T(8,128)(2,1)S(1)}, u32[]{:S(2)}, u32[]{:S(2)}) async-start(bf16[16,8,1536]{2,1,0:T(8,128)(2,1)} %get-tuple-element.31), calls=%async_computation.4 | async-start | bytes 786432 | tf_op jit(solution)/shard_map/all_to_all | solution.py:44
  81.3 2.8 %collective-permute-start.1 = (bf16[256,256]{1,0:T(8,128)(2,1)S(1)}, bf16[256,256]{1,0:T(8,128)(2,1)S(1)}, u32[]{:S(2)}, u32[]{:S(2)}) collective-permute-start(bf16[256,256]{1,0:T(8,128)(2,1)S(1)} %get-tuple-element.20.refs_0_.both_ref), channel_id=1, source_target_pairs={{0,16},{4,20},{8,24},{12,28},{16,32},{20,36},{24,40},{28,44},{32,4... | collective-permute-start | bytes 393224 | tf_op jit(solution)/shard_map/ppermute | solution.py:314
  84.2 3.4 %collective-permute-start = (bf16[256,256]{1,0:T(8,128)(2,1)S(1)}, bf16[256,256]{1,0:T(8,128)(2,1)S(1)}, u32[]{:S(2)}, u32[]{:S(2)}) collective-permute-start(bf16[256,256]{1,0:T(8,128)(2,1)S(1)} %get-tuple-element.20.refs_0_.both_ref), channel_id=1, source_target_pairs={{0,8},{4,12},{8,16},{12,20},{16,24},{20,28},{24,32},{28,36},{32,40... | collective-permute-start | bytes 393224 | tf_op jit(solution)/shard_map/ppermute | solution.py:313
  87.6 0.0 copy-start
  87.6 4.7 %collective-permute-done.1.fourth_ref = bf16[256,256]{1,0:T(8,128)(2,1)S(1)} collective-permute-done((bf16[256,256]{1,0:T(8,128)(2,1)S(1)}, bf16[256,256]{1,0:T(8,128)(2,1)S(1)}, u32[]{:S(2)}, u32[]{:S(2)}) %collective-permute-start.1) | collective-permute-done | bytes 131104 | tf_op jit(solution)/shard_map/ppermute | solution.py:314
  92.3 1.8 %collective-permute-done.second_ref = bf16[256,256]{1,0:T(8,128)(2,1)S(1)} collective-permute-done((bf16[256,256]{1,0:T(8,128)(2,1)S(1)}, bf16[256,256]{1,0:T(8,128)(2,1)S(1)}, u32[]{:S(2)}, u32[]{:S(2)}) %collective-permute-start) | collective-permute-done | bytes 131104 | tf_op jit(solution)/shard_map/ppermute | solution.py:313
  94.0 0.1 maximum_select_fusion
  94.1 3.4 %collective-permute-start.2 = (bf16[512,256]{1,0:T(8,128)(2,1)S(1)}, bf16[512,256]{1,0:T(8,128)(2,1)S(1)}, u32[]{:S(2)}, u32[]{:S(2)}) collective-permute-start(bf16[512,256]{1,0:T(8,128)(2,1)S(1)} %maximum_select_fusion), channel_id=1, source_target_pairs={{0,4},{4,0},{8,12},{12,8},{16,20},{20,16},{24,28},{28,24},{32,36},... | collective-permute-start | bytes 786440 | tf_op jit(solution)/shard_map/ppermute | solution.py:333
  97.5 4.9 %collective-permute-done.2.swapped_ref = bf16[512,256]{1,0:T(8,128)(2,1)S(1)} collective-permute-done((bf16[512,256]{1,0:T(8,128)(2,1)S(1)}, bf16[512,256]{1,0:T(8,128)(2,1)S(1)}, u32[]{:S(2)}, u32[]{:S(2)}) %collective-permute-start.2) | collective-permute-done | bytes 262176 | tf_op jit(solution)/shard_map/ppermute | solution.py:333
  102.4 0.0 copy-done
  102.4 0.8 shard_map.118
  103.1 0.0 all-to-all-done.4
  103.1 1.2 %shard_map.119 = (bf16[128,256]{1,0:T(8,128)(2,1)}, f32[3,2,256]{2,1,0:T(2,128)}, f32[3,2,256]{2,1,0:T(2,128)}) custom-call(f32[1]{0:T(128)S(6)} %copy.12.decay_ref, f32[1,1536]{1,0:T(1,128)S(1)} %get-tuple-element.26.own_ref, f32[3,2,256]{2,1,0:T(2,128)S(1)} %get-tuple-element.27.weights_ref, f32[3,2,256]{2,1,0:T(2,128)S(1)} %get-tuple-element.28.moments_ref, ...), custom_call_target="tpu_custom_call" | custom-call | flops 100000000 | bytes 609284 | tf_op jit(solution)/shard_map/pallas_call | solution.py:268
Async XLA Ops:
  30.5 13.2 %all-to-all-start.1 = ((bf16[16,8,1536]{2,1,0:T(8,128)(2,1)}), bf16[16,8,1536]{2,1,0:T(8,128)(2,1)S(1)}, u32[]{:S(2)}, u32[]{:S(2)}) async-start(bf16[16,8,1536]{2,1,0:T(8,128)(2,1)} %get-tuple-element.24), calls=%async_computation.1 | async-start | bytes 786432 | tf_op jit(solution)/shard_map/all_to_all | solution.py:44
  36.8 0.7 copy-start.1
  56.6 19.1 %all-to-all-start.3 = ((bf16[8,8,1536]{2,1,0:T(8,128)(2,1)}), bf16[8,8,1536]{2,1,0:T(8,128)(2,1)S(1)}, u32[]{:S(2)}, u32[]{:S(2)}) async-start(bf16[8,8,1536]{2,1,0:T(8,128)(2,1)} %shard_map.116), calls=%async_computation.3 | async-start | bytes 393216 | tf_op jit(solution)/shard_map/all_to_all | solution.py:44
  76.6 26.6 %all-to-all-start.4 = ((bf16[16,8,1536]{2,1,0:T(8,128)(2,1)}), bf16[16,8,1536]{2,1,0:T(8,128)(2,1)S(1)}, u32[]{:S(2)}, u32[]{:S(2)}) async-start(bf16[16,8,1536]{2,1,0:T(8,128)(2,1)} %get-tuple-element.31), calls=%async_computation.4 | async-start | bytes 786432 | tf_op jit(solution)/shard_map/all_to_all | solution.py:44
  81.3 10.9 %collective-permute-start.1 = (bf16[256,256]{1,0:T(8,128)(2,1)S(1)}, bf16[256,256]{1,0:T(8,128)(2,1)S(1)}, u32[]{:S(2)}, u32[]{:S(2)}) collective-permute-start(bf16[256,256]{1,0:T(8,128)(2,1)S(1)} %get-tuple-element.20.refs_0_.both_ref), channel_id=1, source_target_pairs={{0,16},{4,20},{8,24},{12,28},{16,32},{20,36},{24,40},{28,44},{32,4... | collective-permute-start | bytes 393224 | tf_op jit(solution)/shard_map/ppermute | solution.py:314
  84.2 9.9 %collective-permute-start = (bf16[256,256]{1,0:T(8,128)(2,1)S(1)}, bf16[256,256]{1,0:T(8,128)(2,1)S(1)}, u32[]{:S(2)}, u32[]{:S(2)}) collective-permute-start(bf16[256,256]{1,0:T(8,128)(2,1)S(1)} %get-tuple-element.20.refs_0_.both_ref), channel_id=1, source_target_pairs={{0,8},{4,12},{8,16},{12,20},{16,24},{20,28},{24,32},{28,36},{32,40... | collective-permute-start | bytes 393224 | tf_op jit(solution)/shard_map/ppermute | solution.py:313
  87.6 14.8 %copy-start = (bf16[128,256]{1,0:T(8,128)(2,1)S(1)}, bf16[128,256]{1,0:T(8,128)(2,1)}, u32[]{:S(2)}) copy-start(bf16[128,256]{1,0:T(8,128)(2,1)} %queries_ref.1) | copy-start | bytes 196612
  94.1 8.3 %collective-permute-start.2 = (bf16[512,256]{1,0:T(8,128)(2,1)S(1)}, bf16[512,256]{1,0:T(8,128)(2,1)S(1)}, u32[]{:S(2)}, u32[]{:S(2)}) collective-permute-start(bf16[512,256]{1,0:T(8,128)(2,1)S(1)} %maximum_select_fusion), channel_id=1, source_target_pairs={{0,4},{4,0},{8,12},{12,8},{16,20},{20,16},{24,28},{28,24},{32,36},... | collective-permute-start | bytes 786440 | tf_op jit(solution)/shard_map/ppermute | solution.py:333

commit v2 on v1

--- a/solution.py
+++ b/solution.py
@@ -94,9 +94,19 @@
     return jnp.concatenate([ref[m, e : e + 1, :] for m in range(3) for e in range(2)], axis=1)
 
 
+def send_all(stage_ref, out_hbm, sems):
+    copies = [
+        pltpu.make_async_copy(stage_ref, out_hbm.at[slot], sems.at[slot])
+        for slot in range(out_hbm.shape[0])
+    ]
+    for copy in copies:
+        copy.start()
+    return copies
+
+
 def pack_kernel(
     weights_hbm, moments_hbm, keys_hbm, values_hbm, memory_hbm, window_hbm,
-    out_ref, both_ref, weights_ref, moments_ref, memory_ref, window_ref, sems,
+    out_hbm, both_ref, weights_ref, moments_ref, memory_ref, window_ref, stage_ref, sems, out_sems,
 ):
     moves = (
         (weights_hbm, weights_ref),
@@ -115,8 +125,8 @@
     copies[0].wait()
     copies[1].wait()
     both = jnp.concatenate([flat_rows(weights_ref), flat_rows(moments_ref)], axis=0)
-    out_ref[...] = jnp.broadcast_to(both.astype(jnp.bfloat16)[None], out_ref.shape)
-    for copy in copies[2:]:
+    stage_ref[...] = both.astype(jnp.bfloat16)
+    for copy in send_all(stage_ref, out_hbm, out_sems) + copies[2:]:
         copy.wait()
 
 
@@ -137,33 +147,57 @@
         spread_ref[slot] = weights
 
 
-def gradient_kernel(keys_ref, target_ref, whole_ref, out_ref):
-    order = row_order()
-    keys, target_grad = keys_ref[...], target_ref[...]
-    gate_pre = matmul(keys, matrix_of(whole_ref, 0))
-    up_pre = matmul(keys, matrix_of(whole_ref, 1))
-    down = matmul(order, matrix_of(whole_ref, 2)).astype(jnp.bfloat16)
+def natural_rows(slot, half):
+    y, near = slot // (NEAR // Y_SIZE), slot % (NEAR // Y_SIZE)
+    return pl.ds(y * 2 * Z_SIZE * X_SIZE + near * 2 + half, FAR, stride=NEAR // Y_SIZE * 2)
+
+
+def natural_matrix(whole_ref, index, scratch_ref):
+    for slot in range(NEAR):
+        for half in range(2):
+            first = (2 * index + half) * WIDTH
+            part = whole_ref[slot * FAR : (slot + 1) * FAR, first : first + WIDTH]
+            part = part.astype(jnp.float32)
+            scratch_ref[0, natural_rows(slot, half), :] = part[:, :128]
+            scratch_ref[1, natural_rows(slot, half), :] = part[:, 128:]
+    return jnp.concatenate([scratch_ref[0], scratch_ref[1]], axis=1).astype(jnp.bfloat16)
+
+
+def gradient_kernel(both_ref, keys_ref, target_ref, whole_ref, out_ref, down_ref, *sums):
+    target_grad = target_ref[...]
+    down = natural_matrix(whole_ref, 2, down_ref)
+    gate_pre = matmul(keys_ref[...], matrix_of(whole_ref, 0))
+    up_pre = matmul(keys_ref[...], matrix_of(whole_ref, 1))
+    hidden_grad = contract_columns(target_grad, down)
     sigmoid_x = jax.nn.sigmoid(gate_pre)
     gate_act = gate_pre * sigmoid_x
     hidden = (gate_act * up_pre).astype(jnp.bfloat16)
-    hidden_grad = contract_columns(target_grad, down)
     gate_grad = (hidden_grad * up_pre * silu_slope(gate_pre, sigmoid_x)).astype(jnp.bfloat16)
     up_grad = (hidden_grad * gate_act).astype(jnp.bfloat16)
-    hidden = matmul(hidden, order).astype(jnp.bfloat16)
-    pairs = ((keys, gate_grad), (keys, up_grad), (hidden, target_grad))
-    for index, (left, right) in enumerate(pairs):
-        part = contract_rows(left, right).astype(jnp.bfloat16)
-        out_ref[:, index * 512 : index * 512 + 256] = part[:128]
-        out_ref[:, index * 512 + 256 : index * 512 + 512] = part[128:]
-
-
-def near_sum_kernel(parts_ref, out_ref):
+    keys = both_ref[:TOKENS_HERE, :]
+    pairs = ((hidden, target_grad), (keys, up_grad), (keys, gate_grad))
+    for index, (left, right) in zip((2, 1, 0), pairs):
+        total = contract_rows(left, right)
+        sums[index][0] = total[:, :128]
+        sums[index][1] = total[:, 128:]
+        for slot in range(NEAR):
+            for half in range(2):
+                first = (2 * index + half) * WIDTH
+                part = jnp.concatenate(
+                    [sums[index][lane, natural_rows(slot, half), :] for lane in range(2)], axis=1
+                )
+                out_ref[slot * FAR : (slot + 1) * FAR, first : first + WIDTH] = part.astype(
+                    jnp.bfloat16
+                )
+
+
+def near_sum_kernel(parts_ref, out_hbm, stage_ref, sems):
     total = parts_ref[0].astype(jnp.float32)
     for slot in range(1, NEAR):
         total += parts_ref[slot].astype(jnp.float32)
-    total = total.astype(jnp.bfloat16)
-    for slot in range(FAR):
-        out_ref[slot] = total
+    stage_ref[...] = total.astype(jnp.bfloat16)
+    for copy in send_all(stage_ref, out_hbm, sems):
+        copy.wait()
 
 
 def update_kernel(far_ref, decay_ref, parts_ref, kept_ref, spread_ref, own_ref, gradient_ref):
@@ -221,7 +255,7 @@
 
 def recall_kernel(
     decay_ref, own_ref, weights_ref, moments_ref, queries_ref, whole_ref, attended_ref, gain_ref,
-    out_hbm, weights_hbm, moments_hbm, out_ref, weights_out, moments_out, sems,
+    out_hbm, weights_hbm, moments_hbm, out_ref, weights_out, moments_out, down_ref, sems,
 ):
     decay = decay_ref[0]
     for m in range(3):
@@ -241,7 +275,7 @@
     queries = queries_ref[...]
     gate_out = matmul(queries, matrix_of(whole_ref, 0))
     up_out = matmul(queries, matrix_of(whole_ref, 1))
-    down = matmul(row_order(), matrix_of(whole_ref, 2)).astype(jnp.bfloat16)
+    down = natural_matrix(whole_ref, 2, down_ref)
     inner_act = (gate_out * jax.nn.sigmoid(gate_out) * up_out).astype(jnp.bfloat16)
     recalled = matmul(inner_act, down)
     out_ref[...] = (rms_scale(recalled, gain_ref[...]) + attended_ref[...]).astype(jnp.bfloat16)
@@ -269,7 +303,7 @@
         kernel,
         out_shape=shapes,
         in_specs=specs,
-        out_specs=[out_spec] * len(shapes),
+        out_specs=out_spec if isinstance(out_spec, list) else [out_spec] * len(shapes),
         scratch_shapes=scratch,
         compiler_params=pltpu.CompilerParams(vmem_limit_bytes=8 * 2**20),
         cost_estimate=pl.CostEstimate(flops=flops, bytes_accessed=moved, transcendentals=0),
@@ -307,7 +341,12 @@
                 memory_gain.reshape(1, WIDTH), window_gain.reshape(1, WIDTH),
             ),
         ),
-        scratch=[pltpu.SemaphoreType.DMA((6,))],
+        out_spec=[HBM] + [VMEM] * 5,
+        scratch=[
+            pltpu.VMEM((2, ROW), bf16),
+            pltpu.SemaphoreType.DMA((6,)),
+            pltpu.SemaphoreType.DMA((FAR,)),
+        ],
     )
     line = exchange(packed, FAR_GROUPS)
     second = lax.ppermute(both, "seq", [(i, i + 2) for i in range(seq_count - 2)])
@@ -320,9 +359,22 @@
     )
     sent, kept = call(relay_kernel, [((NEAR, FAR, ROW), bf16), ((FAR, 2 * ROW), f32)], [VMEM], line)
     whole = exchange(sent, NEAR_GROUPS).reshape(seq_count, ROW)
-    partial = call(gradient_kernel, ((seq_count, ROW), bf16), [VMEM] * 3, keys, target_grad, whole)
+    partial = call(
+        gradient_kernel,
+        ((seq_count, ROW), bf16),
+        [VMEM] * 4,
+        both, keys, target_grad, whole,
+        scratch=[pltpu.VMEM((2, WIDTH, 128), f32)] * 4,
+    )
     near_parts = exchange(partial.reshape(NEAR, FAR, ROW), NEAR_GROUPS)
-    near_sum = call(near_sum_kernel, ((FAR, FAR, ROW), bf16), [VMEM], near_parts)
+    near_sum = call(
+        near_sum_kernel,
+        ((FAR, FAR, ROW), bf16),
+        [VMEM],
+        near_parts,
+        out_spec=HBM,
+        scratch=[pltpu.VMEM((FAR, ROW), bf16), pltpu.SemaphoreType.DMA((FAR,))],
+    )
     far_parts = exchange(near_sum, FAR_GROUPS)
     odd = lax.rem(my_index, 2) == 1
     offered = jnp.where(
@@ -356,6 +408,7 @@
             pltpu.VMEM((TOKENS_HERE, WIDTH), bf16),
             pltpu.VMEM(*block),
             pltpu.VMEM(*block),
+            pltpu.VMEM((2, WIDTH, 128), f32),
             pltpu.SemaphoreType.DMA((3,)),
         ],
     )

time: 105 us -> 107 us (1.019)
  waiting for transfers between devices: 32.4 us -> 34.4 us
    ppermute x1, waiting for transfers between devices: 1.77 us -> 3.27 us  [per_device(): lax.ppermute(both, 'seq', [(i, i + 2) for i in range(seq_count - 2)])]
where the time goes in v2:
time: 107 us; the launch traced here: 106 us
  blocking collectives  39.5 us (37%)
  waiting for transfers between devices  34.4 us (32%)
  starting transfers between devices  24.1 us (23%)
  Pallas kernels  6.15 us (6%)
  between operations  1.42 us (1%)
    all_to_all x2, blocking collectives, exchange(): lax.all_to_all(blocks, 'seq', 0, 0, axis_index_groups=groups, tiled=True)  39.5 us
    all_to_all x3, waiting for transfers between devices, exchange(): lax.all_to_all(blocks, 'seq', 0, 0, axis_index_groups=groups, tiled=True)  21.1 us
    all_to_all x3, starting transfers between devices, exchange(): lax.all_to_all(blocks, 'seq', 0, 0, axis_index_groups=groups, tiled=True)  14.5 us
    pallas_call x8, Pallas kernels, call(): pl.pallas_call(kernel, out_shape=shapes, in_specs=specs, out_specs=out_sp...  6.15 us
    ppermute x1, waiting for transfers between devices, per_device(): lax.ppermute(both, 'seq', [(i, i + 4) for i in range(seq_count - 4)])  5.13 us
    ppermute x1, waiting for transfers between devices, per_device(): lax.ppermute(offered, 'seq', [(i, i ^ 1) for i in range(seq_count)])  4.88 us
    ppermute x1, starting transfers between devices, per_device(): lax.ppermute(offered, 'seq', [(i, i ^ 1) for i in range(seq_count)])  3.38 us
    ppermute x1, starting transfers between devices, per_device(): lax.ppermute(both, 'seq', [(i, i + 2) for i in range(seq_count - 2)])  3.37 us
  transfers between devices with their start and end apart: 6, of which 5 were waited for; matrix products, arithmetic and copies ran while one was open for 0% of the time, Pallas kernels for 1%

profile of v2, /device:TPU:8, one launch (start us, length us, event | category | flops | bytes accessed | tf_op | source)
XLA Modules:
  0.0 106.2 jit_solution(18395231080770700227)
XLA Ops:
  0.6 1.0 shard_map.112
  1.7 28.0 %all_to_all.25.line_ref = bf16[8,2,1536]{2,1,0:T(2,128)(2,1)S(1)} all-to-all(bf16[8,2,1536]{2,1,0:T(2,128)(2,1)S(1)} %get-tuple-element.23), channel_id=1, replica_groups={{0,16,32,48,64,80,96,112},{4,20,36,52,68,84,100,116},{8,24,40,56,72,88,..., dimensions={0} | all-to-all | bytes 98304 | tf_op jit(solution)/shard_map/all_to_all | solution.py:44
  29.7 0.8 shard_map.114
  30.5 6.3 %all-to-all-start.1 = ((bf16[16,8,1536]{2,1,0:T(8,128)(2,1)}), bf16[16,8,1536]{2,1,0:T(8,128)(2,1)S(1)}, u32[]{:S(2)}, u32[]{:S(2)}) async-start(bf16[16,8,1536]{2,1,0:T(8,128)(2,1)} %get-tuple-element.24), calls=%async_computation.1 | async-start | bytes 786432 | tf_op jit(solution)/shard_map/all_to_all | solution.py:44
  36.9 0.0 copy-start.1
  36.9 0.6 copy-done.1
  37.5 0.2 shard_map.113
  37.7 6.1 %all-to-all-done.1 = bf16[16,8,1536]{2,1,0:T(8,128)(2,1)S(1)} async-done(((bf16[16,8,1536]{2,1,0:T(8,128)(2,1)}), bf16[16,8,1536]{2,1,0:T(8,128)(2,1)S(1)}, u32[]{:S(2)}, u32[]{:S(2)}) %all-to-all-start.1) | async-done | bytes 393248 | tf_op jit(solution)/shard_map/all_to_all | solution.py:44
  43.8 0.6 shard_map.115
  44.3 11.4 %all_to_all.26.parts_ref = bf16[16,8,1536]{2,1,0:T(8,128)(2,1)S(1)} all-to-all(bf16[16,8,1536]{2,1,0:T(8,128)(2,1)S(1)} %bitcast.14), channel_id=1, replica_groups={{0,4,8,12,128,132,136,140,256,260,264,268,384,388,392,396},{16,20,24,28..., dimensions={0} | all-to-all | bytes 786432 | tf_op jit(solution)/shard_map/all_to_all | solution.py:44
  55.8 0.8 shard_map.116
  56.6 3.4 %all-to-all-start.3 = ((bf16[8,8,1536]{2,1,0:T(8,128)(2,1)}), bf16[8,8,1536]{2,1,0:T(8,128)(2,1)S(1)}, u32[]{:S(2)}, u32[]{:S(2)}) async-start(bf16[8,8,1536]{2,1,0:T(8,128)(2,1)} %shard_map.116), calls=%async_computation.3 | async-start | bytes 393216 | tf_op jit(solution)/shard_map/all_to_all | solution.py:44
  60.7 15.0 %all-to-all-done.3.parts_ref = bf16[8,8,1536]{2,1,0:T(8,128)(2,1)S(1)} async-done(((bf16[8,8,1536]{2,1,0:T(8,128)(2,1)}), bf16[8,8,1536]{2,1,0:T(8,128)(2,1)S(1)}, u32[]{:S(2)}, u32[]{:S(2)}) %all-to-all-start.3) | async-done | bytes 196640 | tf_op jit(solution)/shard_map/all_to_all | solution.py:44
  75.7 0.9 shard_map.117
  76.6 4.8 %all-to-all-start.4 = ((bf16[16,8,1536]{2,1,0:T(8,128)(2,1)}), bf16[16,8,1536]{2,1,0:T(8,128)(2,1)S(1)}, u32[]{:S(2)}, u32[]{:S(2)}) async-start(bf16[16,8,1536]{2,1,0:T(8,128)(2,1)} %get-tuple-element.31), calls=%async_computation.4 | async-start | bytes 786432 | tf_op jit(solution)/shard_map/all_to_all | solution.py:44
  81.4 3.4 %collective-permute-start = (bf16[256,256]{1,0:T(8,128)(2,1)S(1)}, bf16[256,256]{1,0:T(8,128)(2,1)S(1)}, u32[]{:S(2)}, u32[]{:S(2)}) collective-permute-start(bf16[256,256]{1,0:T(8,128)(2,1)S(1)} %get-tuple-element.20.refs_0_.both_ref), channel_id=1, source_target_pairs={{0,8},{4,12},{8,16},{12,20},{16,24},{20,28},{24,32},{28,36},{32,40... | collective-permute-start | bytes 393224 | tf_op jit(solution)/shard_map/ppermute | solution.py:352
  84.8 2.8 %collective-permute-start.1 = (bf16[256,256]{1,0:T(8,128)(2,1)S(1)}, bf16[256,256]{1,0:T(8,128)(2,1)S(1)}, u32[]{:S(2)}, u32[]{:S(2)}) collective-permute-start(bf16[256,256]{1,0:T(8,128)(2,1)S(1)} %get-tuple-element.20.refs_0_.both_ref), channel_id=1, source_target_pairs={{0,16},{4,20},{8,24},{12,28},{16,32},{20,36},{24,40},{28,44},{32,4... | collective-permute-start | bytes 393224 | tf_op jit(solution)/shard_map/ppermute | solution.py:353
  87.6 0.0 copy-start
  87.6 3.3 %collective-permute-done.second_ref = bf16[256,256]{1,0:T(8,128)(2,1)S(1)} collective-permute-done((bf16[256,256]{1,0:T(8,128)(2,1)S(1)}, bf16[256,256]{1,0:T(8,128)(2,1)S(1)}, u32[]{:S(2)}, u32[]{:S(2)}) %collective-permute-start) | collective-permute-done | bytes 131104 | tf_op jit(solution)/shard_map/ppermute | solution.py:352
  90.9 5.1 %collective-permute-done.1.fourth_ref = bf16[256,256]{1,0:T(8,128)(2,1)S(1)} collective-permute-done((bf16[256,256]{1,0:T(8,128)(2,1)S(1)}, bf16[256,256]{1,0:T(8,128)(2,1)S(1)}, u32[]{:S(2)}, u32[]{:S(2)}) %collective-permute-start.1) | collective-permute-done | bytes 131104 | tf_op jit(solution)/shard_map/ppermute | solution.py:353
  96.0 0.1 maximum_select_fusion
  96.1 3.4 %collective-permute-start.2 = (bf16[512,256]{1,0:T(8,128)(2,1)S(1)}, bf16[512,256]{1,0:T(8,128)(2,1)S(1)}, u32[]{:S(2)}, u32[]{:S(2)}) collective-permute-start(bf16[512,256]{1,0:T(8,128)(2,1)S(1)} %maximum_select_fusion), channel_id=1, source_target_pairs={{0,4},{4,0},{8,12},{12,8},{16,20},{20,16},{24,28},{28,24},{32,36},... | collective-permute-start | bytes 786440 | tf_op jit(solution)/shard_map/ppermute | solution.py:385
  99.5 4.9 %collective-permute-done.2.swapped_ref = bf16[512,256]{1,0:T(8,128)(2,1)S(1)} collective-permute-done((bf16[512,256]{1,0:T(8,128)(2,1)S(1)}, bf16[512,256]{1,0:T(8,128)(2,1)S(1)}, u32[]{:S(2)}, u32[]{:S(2)}) %collective-permute-start.2) | collective-permute-done | bytes 262176 | tf_op jit(solution)/shard_map/ppermute | solution.py:385
  104.4 0.0 copy-done
  104.4 0.8 shard_map.118
  105.1 0.0 all-to-all-done.4
  105.1 1.1 %shard_map.119 = (bf16[128,256]{1,0:T(8,128)(2,1)}, f32[3,2,256]{2,1,0:T(2,128)}, f32[3,2,256]{2,1,0:T(2,128)}) custom-call(f32[1]{0:T(128)S(6)} %copy.12.decay_ref, f32[1,1536]{1,0:T(1,128)S(1)} %get-tuple-element.26.own_ref, f32[3,2,256]{2,1,0:T(2,128)S(1)} %get-tuple-element.27.weights_ref, f32[3,2,256]{2,1,0:T(2,128)S(1)} %get-tuple-element.28.moments_ref, ...), custom_call_target="tpu_custom_call" | custom-call | flops 100000000 | bytes 609284 | tf_op jit(solution)/shard_map/pallas_call | solution.py:302
Async XLA Ops:
  30.5 13.2 %all-to-all-start.1 = ((bf16[16,8,1536]{2,1,0:T(8,128)(2,1)}), bf16[16,8,1536]{2,1,0:T(8,128)(2,1)S(1)}, u32[]{:S(2)}, u32[]{:S(2)}) async-start(bf16[16,8,1536]{2,1,0:T(8,128)(2,1)} %get-tuple-element.24), calls=%async_computation.1 | async-start | bytes 786432 | tf_op jit(solution)/shard_map/all_to_all | solution.py:44
  36.9 0.7 copy-start.1
  56.6 19.1 %all-to-all-start.3 = ((bf16[8,8,1536]{2,1,0:T(8,128)(2,1)}), bf16[8,8,1536]{2,1,0:T(8,128)(2,1)S(1)}, u32[]{:S(2)}, u32[]{:S(2)}) async-start(bf16[8,8,1536]{2,1,0:T(8,128)(2,1)} %shard_map.116), calls=%async_computation.3 | async-start | bytes 393216 | tf_op jit(solution)/shard_map/all_to_all | solution.py:44
  76.6 28.5 %all-to-all-start.4 = ((bf16[16,8,1536]{2,1,0:T(8,128)(2,1)}), bf16[16,8,1536]{2,1,0:T(8,128)(2,1)S(1)}, u32[]{:S(2)}, u32[]{:S(2)}) async-start(bf16[16,8,1536]{2,1,0:T(8,128)(2,1)} %get-tuple-element.31), calls=%async_computation.4 | async-start | bytes 786432 | tf_op jit(solution)/shard_map/all_to_all | solution.py:44
  81.4 9.5 %collective-permute-start = (bf16[256,256]{1,0:T(8,128)(2,1)S(1)}, bf16[256,256]{1,0:T(8,128)(2,1)S(1)}, u32[]{:S(2)}, u32[]{:S(2)}) collective-permute-start(bf16[256,256]{1,0:T(8,128)(2,1)S(1)} %get-tuple-element.20.refs_0_.both_ref), channel_id=1, source_target_pairs={{0,8},{4,12},{8,16},{12,20},{16,24},{20,28},{24,32},{28,36},{32,40... | collective-permute-start | bytes 393224 | tf_op jit(solution)/shard_map/ppermute | solution.py:352
  84.8 11.3 %collective-permute-start.1 = (bf16[256,256]{1,0:T(8,128)(2,1)S(1)}, bf16[256,256]{1,0:T(8,128)(2,1)S(1)}, u32[]{:S(2)}, u32[]{:S(2)}) collective-permute-start(bf16[256,256]{1,0:T(8,128)(2,1)S(1)} %get-tuple-element.20.refs_0_.both_ref), channel_id=1, source_target_pairs={{0,16},{4,20},{8,24},{12,28},{16,32},{20,36},{24,40},{28,44},{32,4... | collective-permute-start | bytes 393224 | tf_op jit(solution)/shard_map/ppermute | solution.py:353
  87.6 16.8 %copy-start = (bf16[128,256]{1,0:T(8,128)(2,1)S(1)}, bf16[128,256]{1,0:T(8,128)(2,1)}, u32[]{:S(2)}) copy-start(bf16[128,256]{1,0:T(8,128)(2,1)} %queries_ref.1) | copy-start | bytes 196612
  96.1 8.3 %collective-permute-start.2 = (bf16[512,256]{1,0:T(8,128)(2,1)S(1)}, bf16[512,256]{1,0:T(8,128)(2,1)S(1)}, u32[]{:S(2)}, u32[]{:S(2)}) collective-permute-start(bf16[512,256]{1,0:T(8,128)(2,1)S(1)} %maximum_select_fusion), channel_id=1, source_target_pairs={{0,4},{4,0},{8,12},{12,8},{16,20},{20,16},{24,28},{28,24},{32,36},... | collective-permute-start | bytes 786440 | tf_op jit(solution)/shard_map/ppermute | solution.py:385

commit v3 on v2

--- a/solution.py
+++ b/solution.py
@@ -37,6 +37,11 @@
     for y in range(Y_SIZE)
     for p in range(NEAR_Z)
     for x in range(X_SIZE)
+]
+
+
+REDUCE_GROUPS = [
+    [g[i] for i in ((0, 4, 2, 6, 1, 5, 3, 7), (1, 5, 3, 7, 0, 4, 2, 6))[j // X_SIZE % NEAR_Z]] for j, g in enumerate(FAR_GROUPS)
 ]
 
 
@@ -191,13 +196,13 @@
                 )
 
 
-def near_sum_kernel(parts_ref, out_hbm, stage_ref, sems):
+def near_sum_kernel(parts_ref, out_ref):
     total = parts_ref[0].astype(jnp.float32)
     for slot in range(1, NEAR):
         total += parts_ref[slot].astype(jnp.float32)
-    stage_ref[...] = total.astype(jnp.bfloat16)
-    for copy in send_all(stage_ref, out_hbm, sems):
-        copy.wait()
+    total = total.astype(jnp.bfloat16)
+    for slot in range(FAR):
+        out_ref[slot] = total
 
 
 def update_kernel(far_ref, decay_ref, parts_ref, kept_ref, spread_ref, own_ref, gradient_ref):
@@ -367,15 +372,8 @@
         scratch=[pltpu.VMEM((2, WIDTH, 128), f32)] * 4,
     )
     near_parts = exchange(partial.reshape(NEAR, FAR, ROW), NEAR_GROUPS)
-    near_sum = call(
-        near_sum_kernel,
-        ((FAR, FAR, ROW), bf16),
-        [VMEM],
-        near_parts,
-        out_spec=HBM,
-        scratch=[pltpu.VMEM((FAR, ROW), bf16), pltpu.SemaphoreType.DMA((FAR,))],
-    )
-    far_parts = exchange(near_sum, FAR_GROUPS)
+    near_sum = call(near_sum_kernel, ((FAR, FAR, ROW), bf16), [VMEM], near_parts)
+    far_parts = exchange(near_sum, REDUCE_GROUPS)
     odd = lax.rem(my_index, 2) == 1
     offered = jnp.where(
         odd,

time: 107 us -> 104 us (0.972)
  the two profiles are of different devices: /device:TPU:8 before, /device:TPU:10 now
where the time goes in v3:
time: 104 us
  blocking collectives  39.5 us (38%)
  waiting for transfers between devices  31.1 us (30%)
  starting transfers between devices  24.7 us (24%)
  Pallas kernels  6.08 us (6%)
  between operations  1.41 us (1%)
    all_to_all x2, blocking collectives, exchange(): lax.all_to_all(blocks, 'seq', 0, 0, axis_index_groups=groups, tiled=True)  39.5 us
    all_to_all x3, waiting for transfers between devices, exchange(): lax.all_to_all(blocks, 'seq', 0, 0, axis_index_groups=groups, tiled=True)  17.5 us
    all_to_all x3, starting transfers between devices, exchange(): lax.all_to_all(blocks, 'seq', 0, 0, axis_index_groups=groups, tiled=True)  15.4 us
    pallas_call x8, Pallas kernels, call(): pl.pallas_call(kernel, out_shape=shapes, in_specs=specs, out_specs=out_sp...  6.08 us
    ppermute x1, waiting for transfers between devices, per_device(): lax.ppermute(offered, 'seq', [(i, i ^ 1) for i in range(seq_count)])  5.84 us
    ppermute x1, waiting for transfers between devices, per_device(): lax.ppermute(both, 'seq', [(i, i + 4) for i in range(seq_count - 4)])  5.01 us
    ppermute x1, starting transfers between devices, per_device(): lax.ppermute(both, 'seq', [(i, i + 4) for i in range(seq_count - 4)])  3.57 us
    ppermute x1, starting transfers between devices, per_device(): lax.ppermute(both, 'seq', [(i, i + 2) for i in range(seq_count - 2)])  3.37 us
  transfers between devices with their start and end apart: 6, of which 5 were waited for; matrix products, arithmetic and copies ran while one was open for 0% of the time, Pallas kernels for 1%

profile of v3, /device:TPU:10, one launch (start us, length us, event | category | flops | bytes accessed | tf_op | source)
XLA Modules:
  0.0 103.5 jit_solution(2181020272722456337)
XLA Ops:
  0.6 1.0 shard_map.112
  1.7 28.0 %all_to_all.25.line_ref = bf16[8,2,1536]{2,1,0:T(2,128)(2,1)S(1)} all-to-all(bf16[8,2,1536]{2,1,0:T(2,128)(2,1)S(1)} %get-tuple-element.23), channel_id=1, replica_groups={{0,16,32,48,64,80,96,112},{4,20,36,52,68,84,100,116},{8,24,40,56,72,88,..., dimensions={0} | all-to-all | bytes 98304 | tf_op jit(solution)/shard_map/all_to_all | solution.py:49
  29.7 0.8 shard_map.114
  30.5 6.3 %all-to-all-start.1 = ((bf16[16,8,1536]{2,1,0:T(8,128)(2,1)}), bf16[16,8,1536]{2,1,0:T(8,128)(2,1)S(1)}, u32[]{:S(2)}, u32[]{:S(2)}) async-start(bf16[16,8,1536]{2,1,0:T(8,128)(2,1)} %get-tuple-element.24), calls=%async_computation.1 | async-start | bytes 786432 | tf_op jit(solution)/shard_map/all_to_all | solution.py:49
  36.8 0.0 copy-start.1
  36.8 0.6 copy-done.1
  37.5 0.2 shard_map.113
  37.7 5.2 %all-to-all-done.1 = bf16[16,8,1536]{2,1,0:T(8,128)(2,1)S(1)} async-done(((bf16[16,8,1536]{2,1,0:T(8,128)(2,1)}), bf16[16,8,1536]{2,1,0:T(8,128)(2,1)S(1)}, u32[]{:S(2)}, u32[]{:S(2)}) %all-to-all-start.1) | async-done | bytes 393248 | tf_op jit(solution)/shard_map/all_to_all | solution.py:49
  42.9 0.6 shard_map.115
  43.4 11.4 %all_to_all.26.parts_ref = bf16[16,8,1536]{2,1,0:T(8,128)(2,1)S(1)} all-to-all(bf16[16,8,1536]{2,1,0:T(8,128)(2,1)S(1)} %bitcast.14), channel_id=1, replica_groups={{0,4,8,12,128,132,136,140,256,260,264,268,384,388,392,396},{16,20,24,28..., dimensions={0} | all-to-all | bytes 786432 | tf_op jit(solution)/shard_map/all_to_all | solution.py:49
  54.9 0.7 shard_map.116
  55.6 3.4 %all-to-all-start.3 = ((bf16[8,8,1536]{2,1,0:T(8,128)(2,1)}), bf16[8,8,1536]{2,1,0:T(8,128)(2,1)S(1)}, u32[]{:S(2)}, u32[]{:S(2)}) async-start(bf16[8,8,1536]{2,1,0:T(8,128)(2,1)} %shard_map.116), calls=%async_computation.3 | async-start | bytes 393216 | tf_op jit(solution)/shard_map/all_to_all | solution.py:49
  59.7 12.3 %all-to-all-done.3.parts_ref = bf16[8,8,1536]{2,1,0:T(8,128)(2,1)S(1)} async-done(((bf16[8,8,1536]{2,1,0:T(8,128)(2,1)}), bf16[8,8,1536]{2,1,0:T(8,128)(2,1)S(1)}, u32[]{:S(2)}, u32[]{:S(2)}) %all-to-all-start.3) | async-done | bytes 196640 | tf_op jit(solution)/shard_map/all_to_all | solution.py:49
  72.0 0.9 shard_map.117
  72.9 5.7 %all-to-all-start.4 = ((bf16[16,8,1536]{2,1,0:T(8,128)(2,1)}), bf16[16,8,1536]{2,1,0:T(8,128)(2,1)S(1)}, u32[]{:S(2)}, u32[]{:S(2)}) async-start(bf16[16,8,1536]{2,1,0:T(8,128)(2,1)} %get-tuple-element.31), calls=%async_computation.4 | async-start | bytes 786432 | tf_op jit(solution)/shard_map/all_to_all | solution.py:49
  78.6 3.4 %collective-permute-start = (bf16[256,256]{1,0:T(8,128)(2,1)S(1)}, bf16[256,256]{1,0:T(8,128)(2,1)S(1)}, u32[]{:S(2)}, u32[]{:S(2)}) collective-permute-start(bf16[256,256]{1,0:T(8,128)(2,1)S(1)} %get-tuple-element.20.refs_0_.both_ref), channel_id=1, source_target_pairs={{0,8},{4,12},{8,16},{12,20},{16,24},{20,28},{24,32},{28,36},{32,40... | collective-permute-start | bytes 393224 | tf_op jit(solution)/shard_map/ppermute | solution.py:357
  82.0 3.6 %collective-permute-start.1 = (bf16[256,256]{1,0:T(8,128)(2,1)S(1)}, bf16[256,256]{1,0:T(8,128)(2,1)S(1)}, u32[]{:S(2)}, u32[]{:S(2)}) collective-permute-start(bf16[256,256]{1,0:T(8,128)(2,1)S(1)} %get-tuple-element.20.refs_0_.both_ref), channel_id=1, source_target_pairs={{0,16},{4,20},{8,24},{12,28},{16,32},{20,36},{24,40},{28,44},{32,4... | collective-permute-start | bytes 393224 | tf_op jit(solution)/shard_map/ppermute | solution.py:358
  85.6 0.0 copy-start
  85.6 2.7 %collective-permute-done.second_ref = bf16[256,256]{1,0:T(8,128)(2,1)S(1)} collective-permute-done((bf16[256,256]{1,0:T(8,128)(2,1)S(1)}, bf16[256,256]{1,0:T(8,128)(2,1)S(1)}, u32[]{:S(2)}, u32[]{:S(2)}) %collective-permute-start) | collective-permute-done | bytes 131104 | tf_op jit(solution)/shard_map/ppermute | solution.py:357
  88.3 5.0 %collective-permute-done.1.fourth_ref = bf16[256,256]{1,0:T(8,128)(2,1)S(1)} collective-permute-done((bf16[256,256]{1,0:T(8,128)(2,1)S(1)}, bf16[256,256]{1,0:T(8,128)(2,1)S(1)}, u32[]{:S(2)}, u32[]{:S(2)}) %collective-permute-start.1) | collective-permute-done | bytes 131104 | tf_op jit(solution)/shard_map/ppermute | solution.py:358
  93.3 0.1 maximum_select_fusion
  93.4 2.4 %collective-permute-start.2 = (bf16[512,256]{1,0:T(8,128)(2,1)S(1)}, bf16[512,256]{1,0:T(8,128)(2,1)S(1)}, u32[]{:S(2)}, u32[]{:S(2)}) collective-permute-start(bf16[512,256]{1,0:T(8,128)(2,1)S(1)} %maximum_select_fusion), channel_id=1, source_target_pairs={{0,4},{4,0},{8,12},{12,8},{16,20},{20,16},{24,28},{28,24},{32,36},... | collective-permute-start | bytes 786440 | tf_op jit(solution)/shard_map/ppermute | solution.py:383
  95.8 5.8 %collective-permute-done.2.swapped_ref = bf16[512,256]{1,0:T(8,128)(2,1)S(1)} collective-permute-done((bf16[512,256]{1,0:T(8,128)(2,1)S(1)}, bf16[512,256]{1,0:T(8,128)(2,1)S(1)}, u32[]{:S(2)}, u32[]{:S(2)}) %collective-permute-start.2) | collective-permute-done | bytes 262176 | tf_op jit(solution)/shard_map/ppermute | solution.py:383
  101.7 0.0 copy-done
  101.7 0.8 shard_map.118
  102.4 0.0 all-to-all-done.4
  102.4 1.1 %shard_map.119 = (bf16[128,256]{1,0:T(8,128)(2,1)}, f32[3,2,256]{2,1,0:T(2,128)}, f32[3,2,256]{2,1,0:T(2,128)}) custom-call(f32[1]{0:T(128)S(6)} %copy.12.decay_ref, f32[1,1536]{1,0:T(1,128)S(1)} %get-tuple-element.26.own_ref, f32[3,2,256]{2,1,0:T(2,128)S(1)} %get-tuple-element.27.weights_ref, f32[3,2,256]{2,1,0:T(2,128)S(1)} %get-tuple-element.28.moments_ref, ...), custom_call_target="tpu_custom_call" | custom-call | flops 100000000 | bytes 609284 | tf_op jit(solution)/shard_map/pallas_call | solution.py:307
Async XLA Ops:
  30.5 12.3 %all-to-all-start.1 = ((bf16[16,8,1536]{2,1,0:T(8,128)(2,1)}), bf16[16,8,1536]{2,1,0:T(8,128)(2,1)S(1)}, u32[]{:S(2)}, u32[]{:S(2)}) async-start(bf16[16,8,1536]{2,1,0:T(8,128)(2,1)} %get-tuple-element.24), calls=%async_computation.1 | async-start | bytes 786432 | tf_op jit(solution)/shard_map/all_to_all | solution.py:49
  36.8 0.7 copy-start.1
  55.6 16.4 %all-to-all-start.3 = ((bf16[8,8,1536]{2,1,0:T(8,128)(2,1)}), bf16[8,8,1536]{2,1,0:T(8,128)(2,1)S(1)}, u32[]{:S(2)}, u32[]{:S(2)}) async-start(bf16[8,8,1536]{2,1,0:T(8,128)(2,1)} %shard_map.116), calls=%async_computation.3 | async-start | bytes 393216 | tf_op jit(solution)/shard_map/all_to_all | solution.py:49
  72.9 29.5 %all-to-all-start.4 = ((bf16[16,8,1536]{2,1,0:T(8,128)(2,1)}), bf16[16,8,1536]{2,1,0:T(8,128)(2,1)S(1)}, u32[]{:S(2)}, u32[]{:S(2)}) async-start(bf16[16,8,1536]{2,1,0:T(8,128)(2,1)} %get-tuple-element.31), calls=%async_computation.4 | async-start | bytes 786432 | tf_op jit(solution)/shard_map/all_to_all | solution.py:49
  78.6 9.7 %collective-permute-start = (bf16[256,256]{1,0:T(8,128)(2,1)S(1)}, bf16[256,256]{1,0:T(8,128)(2,1)S(1)}, u32[]{:S(2)}, u32[]{:S(2)}) collective-permute-start(bf16[256,256]{1,0:T(8,128)(2,1)S(1)} %get-tuple-element.20.refs_0_.both_ref), channel_id=1, source_target_pairs={{0,8},{4,12},{8,16},{12,20},{16,24},{20,28},{24,32},{28,36},{32,40... | collective-permute-start | bytes 393224 | tf_op jit(solution)/shard_map/ppermute | solution.py:357
  82.0 11.3 %collective-permute-start.1 = (bf16[256,256]{1,0:T(8,128)(2,1)S(1)}, bf16[256,256]{1,0:T(8,128)(2,1)S(1)}, u32[]{:S(2)}, u32[]{:S(2)}) collective-permute-start(bf16[256,256]{1,0:T(8,128)(2,1)S(1)} %get-tuple-element.20.refs_0_.both_ref), channel_id=1, source_target_pairs={{0,16},{4,20},{8,24},{12,28},{16,32},{20,36},{24,40},{28,44},{32,4... | collective-permute-start | bytes 393224 | tf_op jit(solution)/shard_map/ppermute | solution.py:358
  85.6 16.1 %copy-start = (bf16[128,256]{1,0:T(8,128)(2,1)S(1)}, bf16[128,256]{1,0:T(8,128)(2,1)}, u32[]{:S(2)}) copy-start(bf16[128,256]{1,0:T(8,128)(2,1)} %queries_ref.1) | copy-start | bytes 196612
  93.4 8.3 %collective-permute-start.2 = (bf16[512,256]{1,0:T(8,128)(2,1)S(1)}, bf16[512,256]{1,0:T(8,128)(2,1)S(1)}, u32[]{:S(2)}, u32[]{:S(2)}) collective-permute-start(bf16[512,256]{1,0:T(8,128)(2,1)S(1)} %maximum_select_fusion), channel_id=1, source_target_pairs={{0,4},{4,0},{8,12},{12,8},{16,20},{20,16},{24,28},{28,24},{32,36},... | collective-permute-start | bytes 786440 | tf_op jit(solution)/shard_map/ppermute | solution.py:383

commit v4 on v3

--- a/solution.py
+++ b/solution.py
@@ -40,8 +40,17 @@
 ]
 
 
+def near_at(slot):
+    return (slot ^ (slot >> 1)) ^ (NEAR - 1)
+
+
+NEAR_GROUPS = [[group[near_at(slot)] for slot in range(NEAR)] for group in NEAR_GROUPS]
+FIRST_FAR = 5
+GATHER_GROUPS = [group[FIRST_FAR:] + group[:FIRST_FAR] for group in FAR_GROUPS]
+REDUCE_ORDERS = ((0, 4, 2, 6, 1, 5, 3, 7), (2, 6, 1, 5, 3, 7, 0, 4))
 REDUCE_GROUPS = [
-    [g[i] for i in ((0, 4, 2, 6, 1, 5, 3, 7), (1, 5, 3, 7, 0, 4, 2, 6))[j // X_SIZE % NEAR_Z]] for j, g in enumerate(FAR_GROUPS)
+    [group[i] for i in REDUCE_ORDERS[column // X_SIZE % NEAR_Z]]
+    for column, group in enumerate(FAR_GROUPS)
 ]
 
 
@@ -53,7 +62,7 @@
     column = lax.broadcasted_iota(jnp.int32, (WIDTH, WIDTH), 1)
     row = lax.broadcasted_iota(jnp.int32, (WIDTH, WIDTH), 0)
     half, slot = column // 128, column % 128
-    near, far = slot // FAR, slot % FAR
+    near, far = near_at(slot // FAR), slot % FAR
     x = near % X_SIZE
     p = (near // X_SIZE) % NEAR_Z
     y = near // (X_SIZE * NEAR_Z)
@@ -110,8 +119,9 @@
 
 
 def pack_kernel(
-    weights_hbm, moments_hbm, keys_hbm, values_hbm, memory_hbm, window_hbm,
-    out_hbm, both_ref, weights_ref, moments_ref, memory_ref, window_ref, stage_ref, sems, out_sems,
+    weights_hbm, moments_hbm, keys_hbm, values_hbm, memory_hbm, window_hbm, queries_hbm,
+    out_hbm, both_ref, weights_ref, moments_ref, memory_ref, window_ref, queries_ref,
+    stage_ref, sems, out_sems,
 ):
     moves = (
         (weights_hbm, weights_ref),
@@ -120,6 +130,7 @@
         (values_hbm, both_ref.at[pl.ds(TOKENS_HERE, TOKENS_HERE)]),
         (memory_hbm, memory_ref),
         (window_hbm, window_ref),
+        (queries_hbm, queries_ref),
     )
     copies = [
         pltpu.make_async_copy(source, target, sems.at[i])
@@ -135,15 +146,18 @@
         copy.wait()
 
 
-def prepare_kernel(rate, both_ref, rates_ref, keys_out, target_out):
-    keys_out[...] = matmul(both_ref[:TOKENS_HERE, :], row_order()).astype(jnp.bfloat16)
+def prepare_kernel(rate, both_ref, rates_ref, queries_ref, keys_out, target_out, queries_out):
+    order = row_order()
+    keys_out[...] = matmul(both_ref[:TOKENS_HERE, :], order).astype(jnp.bfloat16)
+    queries_out[...] = matmul(queries_ref[...], order).astype(jnp.bfloat16)
     rates = jnp.transpose(jnp.broadcast_to(rates_ref[...], (TOKENS_HERE, TOKENS_HERE)))
     scale = -(rate * jnp.concatenate([rates, rates], axis=1))
     target_out[...] = (scale * both_ref[TOKENS_HERE:, :].astype(jnp.float32)).astype(jnp.bfloat16)
 
 
 def relay_kernel(line_ref, spread_ref, kept_ref):
-    line = line_ref[...].astype(jnp.float32)
+    first = FAR - FIRST_FAR
+    line = jnp.concatenate([line_ref[first:], line_ref[:first]], axis=0).astype(jnp.float32)
     weights, moments = line[:, 0, :], line[:, 1, :]
     kept_ref[:, :ROW] = weights
     kept_ref[:, ROW:] = moments
@@ -153,7 +167,7 @@
 
 
 def natural_rows(slot, half):
-    y, near = slot // (NEAR // Y_SIZE), slot % (NEAR // Y_SIZE)
+    y, near = near_at(slot) // (NEAR // Y_SIZE), near_at(slot) % (NEAR // Y_SIZE)
     return pl.ds(y * 2 * Z_SIZE * X_SIZE + near * 2 + half, FAR, stride=NEAR // Y_SIZE * 2)
 
 
@@ -226,10 +240,9 @@
 
 def attention_kernel(
     index_ref, queries_ref, both_ref, second_ref, fourth_ref, swapped_ref, gain_ref,
-    out_ref, queries_out,
+    out_ref,
 ):
     queries = queries_ref[...]
-    queries_out[...] = matmul(queries, row_order()).astype(jnp.bfloat16)
     my_index = index_ref[0]
     query = lax.broadcasted_iota(jnp.int32, (TOKENS_HERE, TOKENS_HERE), 0)
     key = lax.broadcasted_iota(jnp.int32, (TOKENS_HERE, TOKENS_HERE), 1)
@@ -335,32 +348,33 @@
     block = ((3, 2, WIDTH), f32)
     line_gain = ((1, WIDTH), f32)
 
-    packed, both, own_weights, own_moments, memory_row, window_row = call(
+    packed, both, own_weights, own_moments, memory_row, window_row, own_queries = call(
         pack_kernel,
-        [((FAR, 2, ROW), bf16), ((2 * TOKENS_HERE, WIDTH), bf16), block, block, line_gain, line_gain],
-        [HBM] * 6,
+        [((FAR, 2, ROW), bf16), ((2 * TOKENS_HERE, WIDTH), bf16), block, block, line_gain, line_gain, ((TOKENS_HERE, WIDTH), bf16)],
+        [HBM] * 7,
         *map(
             stay,
             (
                 fast_weights[0], momentum[0], key_vectors, values,
                 memory_gain.reshape(1, WIDTH), window_gain.reshape(1, WIDTH),
+                queries,
             ),
         ),
-        out_spec=[HBM] + [VMEM] * 5,
+        out_spec=[HBM] + [VMEM] * 6,
         scratch=[
             pltpu.VMEM((2, ROW), bf16),
-            pltpu.SemaphoreType.DMA((6,)),
+            pltpu.SemaphoreType.DMA((7,)),
             pltpu.SemaphoreType.DMA((FAR,)),
         ],
     )
-    line = exchange(packed, FAR_GROUPS)
+    line = exchange(packed, GATHER_GROUPS)
     second = lax.ppermute(both, "seq", [(i, i + 2) for i in range(seq_count - 2)])
     fourth = lax.ppermute(both, "seq", [(i, i + 4) for i in range(seq_count - 4)])
-    keys, target_grad = call(
+    keys, target_grad, queries_ordered = call(
         lambda *refs: prepare_kernel(inner_rate, *refs),
-        [((TOKENS_HERE, WIDTH), bf16)] * 2,
-        [VMEM] * 2,
-        both, step_rates.reshape(1, TOKENS_HERE),
+        [((TOKENS_HERE, WIDTH), bf16)] * 3,
+        [VMEM] * 3,
+        both, step_rates.reshape(1, TOKENS_HERE), own_queries,
     )
     sent, kept = call(relay_kernel, [((NEAR, FAR, ROW), bf16), ((FAR, 2 * ROW), f32)], [VMEM], line)
     whole = exchange(sent, NEAR_GROUPS).reshape(seq_count, ROW)
@@ -381,11 +395,11 @@
         jnp.concatenate([both, second], axis=0),
     )
     swapped = lax.ppermute(offered, "seq", [(i, i ^ 1) for i in range(seq_count)])
-    attended, queries_ordered = call(
+    attended = call(
         attention_kernel,
-        [((TOKENS_HERE, WIDTH), f32), ((TOKENS_HERE, WIDTH), bf16)],
+        ((TOKENS_HERE, WIDTH), f32),
         [SMEM] + [VMEM] * 6,
-        my_index.reshape(1), queries, both, second, fourth, swapped, window_row,
+        my_index.reshape(1), own_queries, both, second, fourth, swapped, window_row,
     )
     renewed, own_gradient = call(
         update_kernel,

time: 104 us -> 102 us (0.981)
  the two profiles are of different devices: /device:TPU:10 before, /device:TPU:40 now
where the time goes in v4:
time: 102 us
  starting transfers between devices  37.5 us (37%)
  blocking collectives  31 us (30%)
  waiting for transfers between devices  25.1 us (25%)
  Pallas kernels  6.15 us (6%)
  between operations  1.37 us (1%)
    all_to_all x2, blocking collectives, exchange(): lax.all_to_all(blocks, 'seq', 0, 0, axis_index_groups=groups, tiled=True)  31 us
    all_to_all x3, starting transfers between devices, exchange(): lax.all_to_all(blocks, 'seq', 0, 0, axis_index_groups=groups, tiled=True)  28.1 us
    all_to_all x3, waiting for transfers between devices, exchange(): lax.all_to_all(blocks, 'seq', 0, 0, axis_index_groups=groups, tiled=True)  11.7 us
    ppermute x1, waiting for transfers between devices, per_device(): lax.ppermute(both, 'seq', [(i, i + 4) for i in range(seq_count - 4)])  6.43 us
    pallas_call x8, Pallas kernels, call(): pl.pallas_call(kernel, out_shape=shapes, in_specs=specs, out_specs=out_sp...  6.15 us
    ppermute x1, waiting for transfers between devices, per_device(): lax.ppermute(offered, 'seq', [(i, i ^ 1) for i in range(seq_count)])  5.79 us
    ppermute x1, starting transfers between devices, per_device(): lax.ppermute(both, 'seq', [(i, i + 4) for i in range(seq_count - 4)])  3.66 us
    ppermute x1, starting transfers between devices, per_device(): lax.ppermute(both, 'seq', [(i, i + 2) for i in range(seq_count - 2)])  3.26 us
  transfers between devices with their start and end apart: 6, of which 5 were waited for; matrix products, arithmetic and copies ran while one was open for 0% of the time, Pallas kernels for 1%

profile of v4, /device:TPU:40, one launch (start us, length us, event | category | flops | bytes accessed | tf_op | source)
XLA Modules:
  0.0 101.8 jit_solution(5530114232166957813)
XLA Ops:
  0.6 1.1 %shard_map.112 = (bf16[8,2,1536]{2,1,0:T(2,128)(2,1)S(1)}, bf16[256,256]{1,0:T(8,128)(2,1)S(1)}, f32[3,2,256]{2,1,0:T(2,128)S(1)}, f32[3,2,256]{2,1,0:T(2,128)S(...) custom-call(f32[3,2,256]{2,1,0:T(2,128)} %bitcast.16, f32[3,2,256]{2,1,0:T(2,128)} %bitcast.17, ...), custom_call_target="tpu_custom_call" | custom-call | flops 100000000 | bytes 210944 | tf_op jit(solution)/shard_map/pallas_call | solution.py:320
  1.7 20.0 %all_to_all.25.line_ref = bf16[8,2,1536]{2,1,0:T(2,128)(2,1)S(1)} all-to-all(bf16[8,2,1536]{2,1,0:T(2,128)(2,1)S(1)} %get-tuple-element.24), channel_id=1, replica_groups={{80,96,112,0,16,32,48,64},{84,100,116,4,20,36,52,68},{88,104,120,8,24,4..., dimensions={0} | all-to-all | bytes 98304 | tf_op jit(solution)/shard_map/all_to_all | solution.py:58
  21.7 0.8 shard_map.114
  22.5 6.7 %all-to-all-start.1 = ((bf16[16,8,1536]{2,1,0:T(8,128)(2,1)}), bf16[16,8,1536]{2,1,0:T(8,128)(2,1)S(1)}, u32[]{:S(2)}, u32[]{:S(2)}) async-start(bf16[16,8,1536]{2,1,0:T(8,128)(2,1)} %get-tuple-element.25), calls=%async_computation.1 | async-start | bytes 786432 | tf_op jit(solution)/shard_map/all_to_all | solution.py:58
  29.3 0.0 copy-start
  29.3 0.6 copy-done
  29.9 0.2 shard_map.113
  30.1 4.4 %all-to-all-done.1 = bf16[16,8,1536]{2,1,0:T(8,128)(2,1)S(1)} async-done(((bf16[16,8,1536]{2,1,0:T(8,128)(2,1)}), bf16[16,8,1536]{2,1,0:T(8,128)(2,1)S(1)}, u32[]{:S(2)}, u32[]{:S(2)}) %all-to-all-start.1) | async-done | bytes 393248 | tf_op jit(solution)/shard_map/all_to_all | solution.py:58
  34.6 0.6 shard_map.115
  35.1 11.0 %all_to_all.26.parts_ref = bf16[16,8,1536]{2,1,0:T(8,128)(2,1)S(1)} all-to-all(bf16[16,8,1536]{2,1,0:T(8,128)(2,1)S(1)} %bitcast.14), channel_id=1, replica_groups={{396,392,384,388,260,256,264,268,12,8,0,4,132,128,136,140},{412,408,400..., dimensions={0} | all-to-all | bytes 786432 | tf_op jit(solution)/shard_map/all_to_all | solution.py:58
  46.2 0.7 shard_map.116
  46.9 12.6 %all-to-all-start.3 = ((bf16[8,8,1536]{2,1,0:T(8,128)(2,1)}), bf16[8,8,1536]{2,1,0:T(8,128)(2,1)S(1)}, u32[]{:S(2)}, u32[]{:S(2)}) async-start(bf16[8,8,1536]{2,1,0:T(8,128)(2,1)} %shard_map.116), calls=%async_computation.3 | async-start | bytes 393216 | tf_op jit(solution)/shard_map/all_to_all | solution.py:58
  60.2 7.2 %all-to-all-done.3.parts_ref = bf16[8,8,1536]{2,1,0:T(8,128)(2,1)S(1)} async-done(((bf16[8,8,1536]{2,1,0:T(8,128)(2,1)}), bf16[8,8,1536]{2,1,0:T(8,128)(2,1)S(1)}, u32[]{:S(2)}, u32[]{:S(2)}) %all-to-all-start.3) | async-done | bytes 196640 | tf_op jit(solution)/shard_map/all_to_all | solution.py:58
  67.4 0.9 shard_map.117
  68.3 8.8 %all-to-all-start.4 = ((bf16[16,8,1536]{2,1,0:T(8,128)(2,1)}), bf16[16,8,1536]{2,1,0:T(8,128)(2,1)S(1)}, u32[]{:S(2)}, u32[]{:S(2)}) async-start(bf16[16,8,1536]{2,1,0:T(8,128)(2,1)} %get-tuple-element.31), calls=%async_computation.4 | async-start | bytes 786432 | tf_op jit(solution)/shard_map/all_to_all | solution.py:58
  77.1 3.3 %collective-permute-start = (bf16[256,256]{1,0:T(8,128)(2,1)S(1)}, bf16[256,256]{1,0:T(8,128)(2,1)S(1)}, u32[]{:S(2)}, u32[]{:S(2)}) collective-permute-start(bf16[256,256]{1,0:T(8,128)(2,1)S(1)} %get-tuple-element.20.refs_0_.both_ref), channel_id=1, source_target_pairs={{0,8},{4,12},{8,16},{12,20},{16,24},{20,28},{24,32},{28,36},{32,40... | collective-permute-start | bytes 393224 | tf_op jit(solution)/shard_map/ppermute | solution.py:371
  80.4 3.7 %collective-permute-start.1 = (bf16[256,256]{1,0:T(8,128)(2,1)S(1)}, bf16[256,256]{1,0:T(8,128)(2,1)S(1)}, u32[]{:S(2)}, u32[]{:S(2)}) collective-permute-start(bf16[256,256]{1,0:T(8,128)(2,1)S(1)} %get-tuple-element.20.refs_0_.both_ref), channel_id=1, source_target_pairs={{0,16},{4,20},{8,24},{12,28},{16,32},{20,36},{24,40},{28,44},{32,4... | collective-permute-start | bytes 393224 | tf_op jit(solution)/shard_map/ppermute | solution.py:372
  84.0 1.2 %collective-permute-done.second_ref = bf16[256,256]{1,0:T(8,128)(2,1)S(1)} collective-permute-done((bf16[256,256]{1,0:T(8,128)(2,1)S(1)}, bf16[256,256]{1,0:T(8,128)(2,1)S(1)}, u32[]{:S(2)}, u32[]{:S(2)}) %collective-permute-start) | collective-permute-done | bytes 131104 | tf_op jit(solution)/shard_map/ppermute | solution.py:371
  85.2 6.4 %collective-permute-done.1.fourth_ref = bf16[256,256]{1,0:T(8,128)(2,1)S(1)} collective-permute-done((bf16[256,256]{1,0:T(8,128)(2,1)S(1)}, bf16[256,256]{1,0:T(8,128)(2,1)S(1)}, u32[]{:S(2)}, u32[]{:S(2)}) %collective-permute-start.1) | collective-permute-done | bytes 131104 | tf_op jit(solution)/shard_map/ppermute | solution.py:372
  91.6 0.1 maximum_select_fusion
  91.7 2.5 %collective-permute-start.2 = (bf16[512,256]{1,0:T(8,128)(2,1)S(1)}, bf16[512,256]{1,0:T(8,128)(2,1)S(1)}, u32[]{:S(2)}, u32[]{:S(2)}) collective-permute-start(bf16[512,256]{1,0:T(8,128)(2,1)S(1)} %maximum_select_fusion), channel_id=1, source_target_pairs={{0,4},{4,0},{8,12},{12,8},{16,20},{20,16},{24,28},{28,24},{32,36},... | collective-permute-start | bytes 786440 | tf_op jit(solution)/shard_map/ppermute | solution.py:397
  94.2 5.8 %collective-permute-done.2.swapped_ref = bf16[512,256]{1,0:T(8,128)(2,1)S(1)} collective-permute-done((bf16[512,256]{1,0:T(8,128)(2,1)S(1)}, bf16[512,256]{1,0:T(8,128)(2,1)S(1)}, u32[]{:S(2)}, u32[]{:S(2)}) %collective-permute-start.2) | collective-permute-done | bytes 262176 | tf_op jit(solution)/shard_map/ppermute | solution.py:397
  100.0 0.8 shard_map.118.attended_ref
  100.8 0.0 all-to-all-done.4
  100.8 1.1 %shard_map.119 = (bf16[128,256]{1,0:T(8,128)(2,1)}, f32[3,2,256]{2,1,0:T(2,128)}, f32[3,2,256]{2,1,0:T(2,128)}) custom-call(f32[1]{0:T(128)S(6)} %copy.12.decay_ref, f32[1,1536]{1,0:T(1,128)S(1)} %get-tuple-element.27.own_ref, f32[3,2,256]{2,1,0:T(2,128)S(1)} %get-tuple-element.28.weights_ref, f32[3,2,256]{2,1,0:T(2,128)S(1)} %get-tuple-element.29.moments_ref, ...), custom_call_target="tpu_custom_call" | custom-call | flops 100000000 | bytes 609284 | tf_op jit(solution)/shard_map/pallas_call | solution.py:320
Async XLA Ops:
  22.5 12.0 %all-to-all-start.1 = ((bf16[16,8,1536]{2,1,0:T(8,128)(2,1)}), bf16[16,8,1536]{2,1,0:T(8,128)(2,1)S(1)}, u32[]{:S(2)}, u32[]{:S(2)}) async-start(bf16[16,8,1536]{2,1,0:T(8,128)(2,1)} %get-tuple-element.25), calls=%async_computation.1 | async-start | bytes 786432 | tf_op jit(solution)/shard_map/all_to_all | solution.py:58
  29.3 0.7 copy-start
  46.9 20.5 %all-to-all-start.3 = ((bf16[8,8,1536]{2,1,0:T(8,128)(2,1)}), bf16[8,8,1536]{2,1,0:T(8,128)(2,1)S(1)}, u32[]{:S(2)}, u32[]{:S(2)}) async-start(bf16[8,8,1536]{2,1,0:T(8,128)(2,1)} %shard_map.116), calls=%async_computation.3 | async-start | bytes 393216 | tf_op jit(solution)/shard_map/all_to_all | solution.py:58
  68.3 32.5 %all-to-all-start.4 = ((bf16[16,8,1536]{2,1,0:T(8,128)(2,1)}), bf16[16,8,1536]{2,1,0:T(8,128)(2,1)S(1)}, u32[]{:S(2)}, u32[]{:S(2)}) async-start(bf16[16,8,1536]{2,1,0:T(8,128)(2,1)} %get-tuple-element.31), calls=%async_computation.4 | async-start | bytes 786432 | tf_op jit(solution)/shard_map/all_to_all | solution.py:58
  77.1 8.1 %collective-permute-start = (bf16[256,256]{1,0:T(8,128)(2,1)S(1)}, bf16[256,256]{1,0:T(8,128)(2,1)S(1)}, u32[]{:S(2)}, u32[]{:S(2)}) collective-permute-start(bf16[256,256]{1,0:T(8,128)(2,1)S(1)} %get-tuple-element.20.refs_0_.both_ref), channel_id=1, source_target_pairs={{0,8},{4,12},{8,16},{12,20},{16,24},{20,28},{24,32},{28,36},{32,40... | collective-permute-start | bytes 393224 | tf_op jit(solution)/shard_map/ppermute | solution.py:371
  80.4 11.3 %collective-permute-start.1 = (bf16[256,256]{1,0:T(8,128)(2,1)S(1)}, bf16[256,256]{1,0:T(8,128)(2,1)S(1)}, u32[]{:S(2)}, u32[]{:S(2)}) collective-permute-start(bf16[256,256]{1,0:T(8,128)(2,1)S(1)} %get-tuple-element.20.refs_0_.both_ref), channel_id=1, source_target_pairs={{0,16},{4,20},{8,24},{12,28},{16,32},{20,36},{24,40},{28,44},{32,4... | collective-permute-start | bytes 393224 | tf_op jit(solution)/shard_map/ppermute | solution.py:372
  91.7 8.3 %collective-permute-start.2 = (bf16[512,256]{1,0:T(8,128)(2,1)S(1)}, bf16[512,256]{1,0:T(8,128)(2,1)S(1)}, u32[]{:S(2)}, u32[]{:S(2)}) collective-permute-start(bf16[512,256]{1,0:T(8,128)(2,1)S(1)} %maximum_select_fusion), channel_id=1, source_target_pairs={{0,4},{4,0},{8,12},{12,8},{16,20},{20,16},{24,28},{28,24},{32,36},... | collective-permute-start | bytes 786440 | tf_op jit(solution)/shard_map/ppermute | solution.py:397

commit v5 on v3

--- a/solution.py
+++ b/solution.py
@@ -40,8 +40,17 @@
 ]
 
 
+def near_at(slot):
+    return (slot ^ (slot >> 1)) ^ (NEAR - 1)
+
+
+NEAR_GROUPS = [[group[near_at(slot)] for slot in range(NEAR)] for group in NEAR_GROUPS]
+FIRST_FAR = 5
+GATHER_GROUPS = [group[FIRST_FAR:] + group[:FIRST_FAR] for group in FAR_GROUPS]
+REDUCE_ORDERS = ((0, 4, 2, 6, 1, 5, 3, 7), (2, 6, 1, 5, 3, 7, 0, 4))
 REDUCE_GROUPS = [
-    [g[i] for i in ((0, 4, 2, 6, 1, 5, 3, 7), (1, 5, 3, 7, 0, 4, 2, 6))[j // X_SIZE % NEAR_Z]] for j, g in enumerate(FAR_GROUPS)
+    [group[i] for i in REDUCE_ORDERS[column // X_SIZE % NEAR_Z]]
+    for column, group in enumerate(FAR_GROUPS)
 ]
 
 
@@ -53,7 +62,7 @@
     column = lax.broadcasted_iota(jnp.int32, (WIDTH, WIDTH), 1)
     row = lax.broadcasted_iota(jnp.int32, (WIDTH, WIDTH), 0)
     half, slot = column // 128, column % 128
-    near, far = slot // FAR, slot % FAR
+    near, far = near_at(slot // FAR), slot % FAR
     x = near % X_SIZE
     p = (near // X_SIZE) % NEAR_Z
     y = near // (X_SIZE * NEAR_Z)
@@ -143,7 +152,8 @@
 
 
 def relay_kernel(line_ref, spread_ref, kept_ref):
-    line = line_ref[...].astype(jnp.float32)
+    first = FAR - FIRST_FAR
+    line = jnp.concatenate([line_ref[first:], line_ref[:first]], axis=0).astype(jnp.float32)
     weights, moments = line[:, 0, :], line[:, 1, :]
     kept_ref[:, :ROW] = weights
     kept_ref[:, ROW:] = moments
@@ -153,7 +163,7 @@
 
 
 def natural_rows(slot, half):
-    y, near = slot // (NEAR // Y_SIZE), slot % (NEAR // Y_SIZE)
+    y, near = near_at(slot) // (NEAR // Y_SIZE), near_at(slot) % (NEAR // Y_SIZE)
     return pl.ds(y * 2 * Z_SIZE * X_SIZE + near * 2 + half, FAR, stride=NEAR // Y_SIZE * 2)
 
 
@@ -251,7 +261,7 @@
         scores.append(jnp.where(allowed, part, jnp.float32(-1e30)))
     scores = jnp.concatenate(scores, axis=1)
     weights = jnp.exp(scores - jnp.max(scores, axis=1, keepdims=True))
-    chances = (weights / jnp.sum(weights, axis=1, keepdims=True)).astype(jnp.bfloat16)
+    chances = (weights * (1.0 / jnp.sum(weights, axis=1, keepdims=True))).astype(jnp.bfloat16)
     context = jnp.concatenate(
         [ref[first + TOKENS_HERE : first + 2 * TOKENS_HERE, :] for _, ref, first in pieces], axis=0
     )
@@ -353,7 +363,7 @@
             pltpu.SemaphoreType.DMA((FAR,)),
         ],
     )
-    line = exchange(packed, FAR_GROUPS)
+    line = exchange(packed, GATHER_GROUPS)
     second = lax.ppermute(both, "seq", [(i, i + 2) for i in range(seq_count - 2)])
     fourth = lax.ppermute(both, "seq", [(i, i + 4) for i in range(seq_count - 4)])
     keys, target_grad = call(

time: 104 us -> 102 us (0.981)
  the two profiles are of different devices: /device:TPU:10 before, /device:TPU:40 now
where the time goes in v5:
time: 102 us
  starting transfers between devices  37.5 us (37%)
  blocking collectives  31 us (30%)
  waiting for transfers between devices  25.1 us (25%)
  Pallas kernels  6.09 us (6%)
  between operations  1.37 us (1%)
    all_to_all x2, blocking collectives, exchange(): lax.all_to_all(blocks, 'seq', 0, 0, axis_index_groups=groups, tiled=True)  31 us
    all_to_all x3, starting transfers between devices, exchange(): lax.all_to_all(blocks, 'seq', 0, 0, axis_index_groups=groups, tiled=True)  28.1 us
    all_to_all x3, waiting for transfers between devices, exchange(): lax.all_to_all(blocks, 'seq', 0, 0, axis_index_groups=groups, tiled=True)  11.7 us
    ppermute x1, waiting for transfers between devices, per_device(): lax.ppermute(both, 'seq', [(i, i + 4) for i in range(seq_count - 4)])  6.43 us
    pallas_call x8, Pallas kernels, call(): pl.pallas_call(kernel, out_shape=shapes, in_specs=specs, out_specs=out_sp...  6.09 us
    ppermute x1, waiting for transfers between devices, per_device(): lax.ppermute(offered, 'seq', [(i, i ^ 1) for i in range(seq_count)])  5.79 us
    ppermute x1, starting transfers between devices, per_device(): lax.ppermute(both, 'seq', [(i, i + 4) for i in range(seq_count - 4)])  3.66 us
    ppermute x1, starting transfers between devices, per_device(): lax.ppermute(both, 'seq', [(i, i + 2) for i in range(seq_count - 2)])  3.26 us
  transfers between devices with their start and end apart: 6, of which 5 were waited for; matrix products, arithmetic and copies ran while one was open for 0% of the time, Pallas kernels for 1%

profile of v5, /device:TPU:40, one launch (start us, length us, event | category | flops | bytes accessed | tf_op | source)
XLA Modules:
  0.0 101.8 jit_solution(16681698016004113419)
XLA Ops:
  0.6 1.0 %shard_map.112 = (bf16[8,2,1536]{2,1,0:T(2,128)(2,1)S(1)}, bf16[256,256]{1,0:T(8,128)(2,1)S(1)}, f32[3,2,256]{2,1,0:T(2,128)S(1)}, f32[3,2,256]{2,1,0:T(2,128)S(...) custom-call(f32[3,2,256]{2,1,0:T(2,128)} %bitcast.16, f32[3,2,256]{2,1,0:T(2,128)} %bitcast.17, ...), custom_call_target="tpu_custom_call" | custom-call | flops 100000000 | bytes 145408 | tf_op jit(solution)/shard_map/pallas_call | solution.py:317
  1.7 20.0 %all_to_all.25.line_ref = bf16[8,2,1536]{2,1,0:T(2,128)(2,1)S(1)} all-to-all(bf16[8,2,1536]{2,1,0:T(2,128)(2,1)S(1)} %get-tuple-element.23), channel_id=1, replica_groups={{80,96,112,0,16,32,48,64},{84,100,116,4,20,36,52,68},{88,104,120,8,24,4..., dimensions={0} | all-to-all | bytes 98304 | tf_op jit(solution)/shard_map/all_to_all | solution.py:58
  21.7 0.8 shard_map.114
  22.5 6.7 %all-to-all-start.1 = ((bf16[16,8,1536]{2,1,0:T(8,128)(2,1)}), bf16[16,8,1536]{2,1,0:T(8,128)(2,1)S(1)}, u32[]{:S(2)}, u32[]{:S(2)}) async-start(bf16[16,8,1536]{2,1,0:T(8,128)(2,1)} %get-tuple-element.24), calls=%async_computation.1 | async-start | bytes 786432 | tf_op jit(solution)/shard_map/all_to_all | solution.py:58
  29.2 0.0 copy-start.1
  29.2 0.6 copy-done.1
  29.9 0.2 shard_map.113
  30.1 4.5 %all-to-all-done.1 = bf16[16,8,1536]{2,1,0:T(8,128)(2,1)S(1)} async-done(((bf16[16,8,1536]{2,1,0:T(8,128)(2,1)}), bf16[16,8,1536]{2,1,0:T(8,128)(2,1)S(1)}, u32[]{:S(2)}, u32[]{:S(2)}) %all-to-all-start.1) | async-done | bytes 393248 | tf_op jit(solution)/shard_map/all_to_all | solution.py:58
  34.5 0.6 shard_map.115
  35.1 11.0 %all_to_all.26.parts_ref = bf16[16,8,1536]{2,1,0:T(8,128)(2,1)S(1)} all-to-all(bf16[16,8,1536]{2,1,0:T(8,128)(2,1)S(1)} %bitcast.14), channel_id=1, replica_groups={{396,392,384,388,260,256,264,268,12,8,0,4,132,128,136,140},{412,408,400..., dimensions={0} | all-to-all | bytes 786432 | tf_op jit(solution)/shard_map/all_to_all | solution.py:58
  46.1 0.7 shard_map.116
  46.9 12.6 %all-to-all-start.3 = ((bf16[8,8,1536]{2,1,0:T(8,128)(2,1)}), bf16[8,8,1536]{2,1,0:T(8,128)(2,1)S(1)}, u32[]{:S(2)}, u32[]{:S(2)}) async-start(bf16[8,8,1536]{2,1,0:T(8,128)(2,1)} %shard_map.116), calls=%async_computation.3 | async-start | bytes 393216 | tf_op jit(solution)/shard_map/all_to_all | solution.py:58
  60.1 7.2 %all-to-all-done.3.parts_ref = bf16[8,8,1536]{2,1,0:T(8,128)(2,1)S(1)} async-done(((bf16[8,8,1536]{2,1,0:T(8,128)(2,1)}), bf16[8,8,1536]{2,1,0:T(8,128)(2,1)S(1)}, u32[]{:S(2)}, u32[]{:S(2)}) %all-to-all-start.3) | async-done | bytes 196640 | tf_op jit(solution)/shard_map/all_to_all | solution.py:58
  67.3 0.9 shard_map.117
  68.2 8.8 %all-to-all-start.4 = ((bf16[16,8,1536]{2,1,0:T(8,128)(2,1)}), bf16[16,8,1536]{2,1,0:T(8,128)(2,1)S(1)}, u32[]{:S(2)}, u32[]{:S(2)}) async-start(bf16[16,8,1536]{2,1,0:T(8,128)(2,1)} %get-tuple-element.31), calls=%async_computation.4 | async-start | bytes 786432 | tf_op jit(solution)/shard_map/all_to_all | solution.py:58
  77.1 3.3 %collective-permute-start = (bf16[256,256]{1,0:T(8,128)(2,1)S(1)}, bf16[256,256]{1,0:T(8,128)(2,1)S(1)}, u32[]{:S(2)}, u32[]{:S(2)}) collective-permute-start(bf16[256,256]{1,0:T(8,128)(2,1)S(1)} %get-tuple-element.20.refs_0_.both_ref), channel_id=1, source_target_pairs={{0,8},{4,12},{8,16},{12,20},{16,24},{20,28},{24,32},{28,36},{32,40... | collective-permute-start | bytes 393224 | tf_op jit(solution)/shard_map/ppermute | solution.py:367
  80.3 3.7 %collective-permute-start.1 = (bf16[256,256]{1,0:T(8,128)(2,1)S(1)}, bf16[256,256]{1,0:T(8,128)(2,1)S(1)}, u32[]{:S(2)}, u32[]{:S(2)}) collective-permute-start(bf16[256,256]{1,0:T(8,128)(2,1)S(1)} %get-tuple-element.20.refs_0_.both_ref), channel_id=1, source_target_pairs={{0,16},{4,20},{8,24},{12,28},{16,32},{20,36},{24,40},{28,44},{32,4... | collective-permute-start | bytes 393224 | tf_op jit(solution)/shard_map/ppermute | solution.py:368
  84.0 0.0 copy-start
  84.0 1.2 %collective-permute-done.second_ref = bf16[256,256]{1,0:T(8,128)(2,1)S(1)} collective-permute-done((bf16[256,256]{1,0:T(8,128)(2,1)S(1)}, bf16[256,256]{1,0:T(8,128)(2,1)S(1)}, u32[]{:S(2)}, u32[]{:S(2)}) %collective-permute-start) | collective-permute-done | bytes 131104 | tf_op jit(solution)/shard_map/ppermute | solution.py:367
  85.2 6.4 %collective-permute-done.1.fourth_ref = bf16[256,256]{1,0:T(8,128)(2,1)S(1)} collective-permute-done((bf16[256,256]{1,0:T(8,128)(2,1)S(1)}, bf16[256,256]{1,0:T(8,128)(2,1)S(1)}, u32[]{:S(2)}, u32[]{:S(2)}) %collective-permute-start.1) | collective-permute-done | bytes 131104 | tf_op jit(solution)/shard_map/ppermute | solution.py:368
  91.6 0.1 maximum_select_fusion
  91.7 2.5 %collective-permute-start.2 = (bf16[512,256]{1,0:T(8,128)(2,1)S(1)}, bf16[512,256]{1,0:T(8,128)(2,1)S(1)}, u32[]{:S(2)}, u32[]{:S(2)}) collective-permute-start(bf16[512,256]{1,0:T(8,128)(2,1)S(1)} %maximum_select_fusion), channel_id=1, source_target_pairs={{0,4},{4,0},{8,12},{12,8},{16,20},{20,16},{24,28},{28,24},{32,36},... | collective-permute-start | bytes 786440 | tf_op jit(solution)/shard_map/ppermute | solution.py:393
  94.2 5.8 %collective-permute-done.2.swapped_ref = bf16[512,256]{1,0:T(8,128)(2,1)S(1)} collective-permute-done((bf16[512,256]{1,0:T(8,128)(2,1)S(1)}, bf16[512,256]{1,0:T(8,128)(2,1)S(1)}, u32[]{:S(2)}, u32[]{:S(2)}) %collective-permute-start.2) | collective-permute-done | bytes 262176 | tf_op jit(solution)/shard_map/ppermute | solution.py:393
  99.9 0.0 copy-done
  99.9 0.8 shard_map.118
  100.7 0.0 all-to-all-done.4
  100.7 1.1 %shard_map.119 = (bf16[128,256]{1,0:T(8,128)(2,1)}, f32[3,2,256]{2,1,0:T(2,128)}, f32[3,2,256]{2,1,0:T(2,128)}) custom-call(f32[1]{0:T(128)S(6)} %copy.12.decay_ref, f32[1,1536]{1,0:T(1,128)S(1)} %get-tuple-element.26.own_ref, f32[3,2,256]{2,1,0:T(2,128)S(1)} %get-tuple-element.27.weights_ref, f32[3,2,256]{2,1,0:T(2,128)S(1)} %get-tuple-element.28.moments_ref, ...), custom_call_target="tpu_custom_call" | custom-call | flops 100000000 | bytes 609284 | tf_op jit(solution)/shard_map/pallas_call | solution.py:317
Async XLA Ops:
  22.5 12.0 %all-to-all-start.1 = ((bf16[16,8,1536]{2,1,0:T(8,128)(2,1)}), bf16[16,8,1536]{2,1,0:T(8,128)(2,1)S(1)}, u32[]{:S(2)}, u32[]{:S(2)}) async-start(bf16[16,8,1536]{2,1,0:T(8,128)(2,1)} %get-tuple-element.24), calls=%async_computation.1 | async-start | bytes 786432 | tf_op jit(solution)/shard_map/all_to_all | solution.py:58
  29.2 0.7 copy-start.1
  46.9 20.5 %all-to-all-start.3 = ((bf16[8,8,1536]{2,1,0:T(8,128)(2,1)}), bf16[8,8,1536]{2,1,0:T(8,128)(2,1)S(1)}, u32[]{:S(2)}, u32[]{:S(2)}) async-start(bf16[8,8,1536]{2,1,0:T(8,128)(2,1)} %shard_map.116), calls=%async_computation.3 | async-start | bytes 393216 | tf_op jit(solution)/shard_map/all_to_all | solution.py:58
  68.2 32.5 %all-to-all-start.4 = ((bf16[16,8,1536]{2,1,0:T(8,128)(2,1)}), bf16[16,8,1536]{2,1,0:T(8,128)(2,1)S(1)}, u32[]{:S(2)}, u32[]{:S(2)}) async-start(bf16[16,8,1536]{2,1,0:T(8,128)(2,1)} %get-tuple-element.31), calls=%async_computation.4 | async-start | bytes 786432 | tf_op jit(solution)/shard_map/all_to_all | solution.py:58
  77.1 8.1 %collective-permute-start = (bf16[256,256]{1,0:T(8,128)(2,1)S(1)}, bf16[256,256]{1,0:T(8,128)(2,1)S(1)}, u32[]{:S(2)}, u32[]{:S(2)}) collective-permute-start(bf16[256,256]{1,0:T(8,128)(2,1)S(1)} %get-tuple-element.20.refs_0_.both_ref), channel_id=1, source_target_pairs={{0,8},{4,12},{8,16},{12,20},{16,24},{20,28},{24,32},{28,36},{32,40... | collective-permute-start | bytes 393224 | tf_op jit(solution)/shard_map/ppermute | solution.py:367
  80.3 11.3 %collective-permute-start.1 = (bf16[256,256]{1,0:T(8,128)(2,1)S(1)}, bf16[256,256]{1,0:T(8,128)(2,1)S(1)}, u32[]{:S(2)}, u32[]{:S(2)}) collective-permute-start(bf16[256,256]{1,0:T(8,128)(2,1)S(1)} %get-tuple-element.20.refs_0_.both_ref), channel_id=1, source_target_pairs={{0,16},{4,20},{8,24},{12,28},{16,32},{20,36},{24,40},{28,44},{32,4... | collective-permute-start | bytes 393224 | tf_op jit(solution)/shard_map/ppermute | solution.py:368
  84.0 16.0 %copy-start = (bf16[128,256]{1,0:T(8,128)(2,1)S(1)}, bf16[128,256]{1,0:T(8,128)(2,1)}, u32[]{:S(2)}) copy-start(bf16[128,256]{1,0:T(8,128)(2,1)} %queries_ref.1) | copy-start | bytes 196612
  91.7 8.3 %collective-permute-start.2 = (bf16[512,256]{1,0:T(8,128)(2,1)S(1)}, bf16[512,256]{1,0:T(8,128)(2,1)S(1)}, u32[]{:S(2)}, u32[]{:S(2)}) collective-permute-start(bf16[512,256]{1,0:T(8,128)(2,1)S(1)} %maximum_select_fusion), channel_id=1, source_target_pairs={{0,4},{4,0},{8,12},{12,8},{16,20},{20,16},{24,28},{28,24},{32,36},... | collective-permute-start | bytes 786440 | tf_op jit(solution)/shard_map/ppermute | solution.py:393
